TPU v7x, 256 devices: a whole 4x4x8 slice. The times are simulated.
256 devices in a mesh: ctx: 32 (over y_lo, z, core), seq: 2 (over y_hi), ch: 4 (over x).
Axes of the slice: x: 4, y: 4 (y_hi: 2, y_lo: 2; y = y_hi * 2 + y_lo), z: 8, core: 2. Of those that a mesh axis runs over, the one named last changes fastest.
Arguments:
- grad_out: float32 [2, 512, 16384], P('seq', 'ch', 'ctx'), may hold values from -6 to 6
- query: float32 [2, 512, 16384], P('seq', 'ch', 'ctx'), may hold values from -6 to 6
- keys: float32 [2, 512, 16384], P('seq', 'ch', 'ctx'), may hold values from -6 to 6
- values: float32 [2, 512, 16384], P('seq', 'ch', 'ctx'), may hold values from -6 to 6
- long_filter: float32 [512, 16384], P(('ch', 'ctx')), may hold values from -6 to 6
- short_filter: float32 [512, 3], P('ch'), may hold values from -3.5 to 3.5
Outputs:
- grad_query: float32 [2, 512, 16384], P('seq', 'ch', 'ctx')
- grad_keys: float32 [2, 512, 16384], P('seq', 'ch', 'ctx')
- grad_values: float32 [2, 512, 16384], P('seq', 'ch', 'ctx')
- grad_long: float32 [512, 16384], P(('ch', 'ctx'))
All inputs are finite; a program needn't handle non-finite values.
Results may differ from a plain program's by a relative error of at most 0.0001.
Values sent between devices are 32-bit elements; how exact they have to be, the bound alone decides.
No kernel may reach another device: no remote copies, remote signals or barrier semaphores. Data moves between devices by JAX's collectives and lax.ppermute only.
A program may use at most 64 MiB of HBM per device.

v0:
```python
import math

import jax
import jax.numpy as jnp
from jax import lax
from jax.sharding import PartitionSpec as P

exact_mode = lax.Precision.HIGHEST


def from_behind(block, axis, distance):
    devices = range(lax.axis_size(axis))
    route = [(i - distance, i) for i in devices if i - distance in devices]
    return lax.ppermute(block, axis, route)


def depthwise(signal, kernel):
    return lax.conv_general_dilated(
        signal,
        kernel[:, None, :],
        (1,),
        "VALID",
        dimension_numbers=("NCH", "OIH", "NCH"),
        feature_group_count=kernel.shape[0],
        precision=exact_mode,
    )


def cos_sin(period, row_count, col_count):
    row_ids = jnp.arange(row_count, dtype=jnp.int32)
    col_ids = jnp.arange(col_count, dtype=jnp.int32)
    phases = (row_ids[:, None] * col_ids[None, :] % period).astype(jnp.float32) * (
        2.0 * math.pi / period
    )
    return (jnp.cos(phases), jnp.sin(phases))


def make_tables(outer_len, inner_len):
    padded_len = outer_len * inner_len
    half_outer = outer_len // 2
    cos_out, sin_out = cos_sin(outer_len, outer_len, half_outer)
    cos_turn, sin_turn = cos_sin(padded_len, outer_len, inner_len)
    cos_in, sin_in = cos_sin(inner_len, inner_len, inner_len)
    outer_fwd = jnp.concatenate([cos_out, -sin_out], axis=0)
    outer_inv = jnp.concatenate([cos_out.T, -sin_out.T], axis=1)
    inner_fwd = jnp.concatenate(
        [jnp.concatenate([cos_in, -sin_in], axis=1), jnp.concatenate([sin_in, cos_in], axis=1)],
        axis=0,
    )
    inner_inv = jnp.concatenate(
        [jnp.concatenate([cos_in, sin_in], axis=1), jnp.concatenate([-sin_in, cos_in], axis=1)],
        axis=0,
    )
    return (outer_fwd, outer_inv, inner_fwd, inner_inv, cos_turn[:, None, :], sin_turn[:, None, :])


def spectrum(signal, tables):
    outer_fwd, outer_inv, inner_fwd, inner_inv, cos_turn, sin_turn = tables
    outer_len = outer_fwd.shape[0] // 2
    inner_len = cos_turn.shape[2]
    row_count = signal.shape[0]
    folded = signal.reshape(row_count, outer_len // 2, inner_len)
    section = jnp.einsum("kt,rtb->krb", outer_fwd, folded, precision=exact_mode)
    section_re = section[:outer_len]
    section_im = section[outer_len:]
    turned_re = section_re * cos_turn + section_im * sin_turn
    turned_im = section_im * cos_turn - section_re * sin_turn
    joined = jnp.concatenate([turned_re, turned_im], axis=2)
    spec = jnp.dot(
        joined.reshape(outer_len * row_count, 2 * inner_len), inner_fwd, precision=exact_mode
    )
    spec = spec.reshape(outer_len, row_count, 2 * inner_len)
    return (spec[:, :, :inner_len], spec[:, :, inner_len:])


def inverse(spec_re, spec_im, tables):
    outer_fwd, outer_inv, inner_fwd, inner_inv, cos_turn, sin_turn = tables
    outer_len, row_count, inner_len = spec_re.shape
    padded_len = outer_len * inner_len
    joined = jnp.concatenate([spec_re, spec_im], axis=2)
    back = jnp.dot(
        joined.reshape(outer_len * row_count, 2 * inner_len), inner_inv, precision=exact_mode
    )
    back = back.reshape(outer_len, row_count, 2 * inner_len)
    back_re = back[:, :, :inner_len]
    back_im = back[:, :, inner_len:]
    turned_re = back_re * cos_turn - back_im * sin_turn
    turned_im = back_re * sin_turn + back_im * cos_turn
    stacked = jnp.concatenate([turned_re, turned_im], axis=0)
    signal = jnp.einsum("tk,krb->rtb", outer_inv, stacked, precision=exact_mode)
    return signal.reshape(row_count, outer_len // 2 * inner_len) / padded_len


def long_terms(gated_own, grad_own, own_filter):
    seq_here, own_chans, length = gated_own.shape
    padded_len = 2 * length
    outer_len = 2 ** ((padded_len.bit_length() - 1) // 2)
    inner_len = padded_len // outer_len
    tables = make_tables(outer_len, inner_len)
    scale_factor = length ** (-0.5)
    many = seq_here * own_chans
    stacked = jnp.concatenate(
        [gated_own.reshape(many, length), grad_own.reshape(many, length), own_filter], axis=0
    )
    spec_re, spec_im = spectrum(stacked, tables)
    grid = (outer_len, seq_here, own_chans, inner_len)
    fgrid = (outer_len, 1, own_chans, inner_len)
    gate_re = spec_re[:, :many].reshape(grid)
    gate_im = spec_im[:, :many].reshape(grid)
    grad_re = spec_re[:, many : 2 * many].reshape(grid)
    grad_im = spec_im[:, many : 2 * many].reshape(grid)
    filt_re = spec_re[:, 2 * many :].reshape(fgrid)
    filt_im = spec_im[:, 2 * many :].reshape(fgrid)
    out_re = gate_re * filt_re - gate_im * filt_im
    out_im = gate_re * filt_im + gate_im * filt_re
    back_re = grad_re * filt_re + grad_im * filt_im
    back_im = grad_im * filt_re - grad_re * filt_im
    cross_re = jnp.sum(grad_re * gate_re + grad_im * gate_im, axis=1)
    cross_im = jnp.sum(grad_im * gate_re - grad_re * gate_im, axis=1)
    flat = (outer_len, many, inner_len)
    all_re = jnp.concatenate([out_re.reshape(flat), back_re.reshape(flat), cross_re], axis=1)
    all_im = jnp.concatenate([out_im.reshape(flat), back_im.reshape(flat), cross_im], axis=1)
    signals = inverse(all_re, all_im, tables)[:, :length] * scale_factor
    conv_own = signals[:many].reshape(seq_here, own_chans, length)
    grad_gated_own = signals[many : 2 * many].reshape(seq_here, own_chans, length)
    filter_part = signals[2 * many :]
    return (conv_own, grad_gated_own, filter_part)


def shards(grad_out, query, keys, values, long_filter, short_filter):
    tap_count = short_filter.shape[1]
    tok_width = keys.shape[2]
    key_tail = keys[:, :, tok_width - tap_count :]
    key_before = from_behind(key_tail, "ctx", 1)
    key_window = jnp.concatenate([key_before[:, :, 1:], keys], axis=2)
    short_keys = depthwise(key_window, jnp.flip(short_filter, 1))
    gated = short_keys * values
    grad_conv = grad_out * query
    gated_own, grad_own = (
        lax.all_to_all(gated, "ctx", split_axis=1, concat_axis=2, tiled=True),
        lax.all_to_all(grad_conv, "ctx", split_axis=1, concat_axis=2, tiled=True),
    )
    conv_own, grad_gated_own, filter_part = long_terms(gated_own, grad_own, long_filter)
    conv_tok, grad_gated = (
        lax.all_to_all(conv_own, "ctx", split_axis=2, concat_axis=1, tiled=True),
        lax.all_to_all(grad_gated_own, "ctx", split_axis=2, concat_axis=1, tiled=True),
    )
    grad_long = lax.psum(filter_part, "seq")
    grad_query = grad_out * conv_tok
    grad_short = grad_gated * values
    grad_values = grad_gated * short_keys
    grad_head = grad_short[:, :, :tap_count]
    grad_after = from_behind(grad_head, "ctx", -1)
    grad_window = jnp.concatenate([grad_short, grad_after[:, :, : tap_count - 1]], axis=2)
    grad_keys = depthwise(grad_window, short_filter)
    return (grad_query, grad_keys, grad_values, grad_long)


def solution(mesh):
    return jax.shard_map(
        shards,
        mesh=mesh,
        in_specs=(
            P("seq", "ch", "ctx"),
            P("seq", "ch", "ctx"),
            P("seq", "ch", "ctx"),
            P("seq", "ch", "ctx"),
            P(("ch", "ctx"), None),
            P("ch", None),
        ),
        out_specs=(
            P("seq", "ch", "ctx"),
            P("seq", "ch", "ctx"),
            P("seq", "ch", "ctx"),
            P(("ch", "ctx"), None),
        ),
        check_vma=False,
    )
```

profile of v0, /device:TPU:1, one launch (start us, length us, event | category | flops | bytes accessed | tf_op | source)
XLA Modules:
  0.0 321.9 jit_solution(12230810290048559770)
XLA Ops:
  7.2 0.9 slice.64
  8.1 4.9 %collective-permute-start = (f32[1,128,3]{2,1,0:T(8,128)S(1)}, f32[1,128,3]{2,1,0:T(8,128)S(1)}, u32[]{:S(2)}, u32[]{:S(2)}) collective-permute-start(f32[1,128,3]{2,1,0:T(8,128)S(1)} %slice.64), channel_id=1, source_target_pairs={{0,8},{8,16},{16,24},{24,32},{32,40},{40,48},{48,56},{56,64},{64,7... | collective-permute-start | bytes 4616 | tf_op jit(solution)/shard_map/ppermute | solution.py:14
  13.0 1.1 mul.356
  14.1 1.0 copy.125
  15.1 8.8 %all-to-all-start.1 = ((f32[1,128,512]{2,0,1:T(1,128)}), f32[1,128,512]{2,0,1:T(1,128)S(1)}, u32[]{:S(2)}, u32[]{:S(2)}) async-start(f32[1,128,512]{2,0,1:T(1,128)} %copy.125), calls=%async_computation.1 | async-start | bytes 524288 | tf_op jit(solution)/shard_map/all_to_all | solution.py:141
  24.6 1.1 copy.122
  25.8 1.1 maximum_bitcast_fusion
  28.5 7.0 %all-to-all-done.1 = f32[1,128,512]{2,0,1:T(1,128)S(1)} async-done(((f32[1,128,512]{2,0,1:T(1,128)}), f32[1,128,512]{2,0,1:T(1,128)S(1)}, u32[]{:S(2)}, u32[]{:S(2)}) %all-to-all-start.1) | async-done | bytes 262176 | tf_op jit(solution)/shard_map/all_to_all | solution.py:141
  35.5 5.7 %all-to-all-start = ((f32[1,128,512]{2,0,1:T(1,128)}), f32[1,128,512]{2,0,1:T(1,128)S(1)}, u32[]{:S(2)}, u32[]{:S(2)}) async-start(f32[1,128,512]{2,0,1:T(1,128)} %copy.123), calls=%async_computation | async-start | bytes 524288 | tf_op jit(solution)/shard_map/all_to_all | solution.py:140
  41.5 1.0 fusion.70
  43.0 1.0 fusion.65
  44.2 8.5 %all-to-all-done = f32[1,128,512]{2,0,1:T(1,128)S(1)} async-done(((f32[1,128,512]{2,0,1:T(1,128)}), f32[1,128,512]{2,0,1:T(1,128)S(1)}, u32[]{:S(2)}, u32[]{:S(2)}) %all-to-all-start) | async-done | bytes 262176 | tf_op jit(solution)/shard_map/all_to_all | solution.py:140
  52.9 2.7 fusion.36
  56.0 5.2 %fusion = f32[128,12,512]{2,0,1:T(8,128)S(1)} fusion(f32[128,12,256]{0,2,1:T(8,128)S(1)} %get-tuple-element.27, f32[128,12,256]{0,2,1:T(8,128)S(1)} %get-tuple-element.26, f32[256,256]{1,0:T(8,128)S(1)} %get-tuple-element.42, f32[256,256]{1,0:T(8,128)S(1)} %get-tuple-element.41, f32[256,256]{1,0:T(8,128)S(1)} %fusion.70), kind=kOutput, calls=%fused_computation | convolution fusion | flops 4833411072 | bytes 7077888 | tf_op jit(solution)/shard_map/dot_general | solution.py:69
  62.3 5.7 %fusion.4 = f32[128,12,512]{0,2,1:T(8,128)S(1)} fusion(f32[128,4,256]{2,0,1:T(8,128)S(1)} %get-tuple-element.33, f32[128,4,256]{2,0,1:T(8,128)S(1)} %get-tuple-element.32, f32[128,4,256]{2,0,1:T(8,128)S(1)} %get-tuple-element.31, f32[128,4,256]{2,0,1:T(8,128)S(1)} %get-tuple-element.30, f32[128,4,256]{2,0,1:T(8,128)S(1)} %get-tuple-element.29, ...), kind=kOutput, calls=%fused_computation.4 | convolution fusion | flops 4836556800 | bytes 7077888 | tf_op jit(solution)/shard_map/dot_general | solution.py:81
  68.4 3.2 fusion.23
  71.6 4.6 %copy.149 = f32[4,64,256]{0,2,1:T(8,128)} copy(f32[4,64,256]{2,1,0:T(8,128)S(1)} %get-tuple-element.35) | data formatting | bytes 524288 | tf_op jit(solution)/shard_map/reshape | solution.py:125
  76.8 74.7 %reduce.2 = f32[16384,4]{1,0:T(8,128)} reduce(f32[16384,1,4]{2,1,0:T(1,128)} %bitcast.68, f32[]{:T(128)} %broadcast.144), dimensions={1}, to_apply=%bitcast.63.reduce_sub_computation | reduce | bytes 524292
  151.4 9.1 %reshape.140 = f32[32,1,2048]{2,1,0:T(1,128)} reshape(f32[16384,4]{1,0:T(8,128)} %reduce.2) | data formatting | bytes 524288
  160.5 5.1 %all-to-all-start.3 = ((f32[32,1,2048]{2,1,0:T(1,128)}), f32[32,1,2048]{2,1,0:T(1,128)S(1)}, u32[]{:S(2)}, u32[]{:S(2)}) async-start(f32[32,1,2048]{2,1,0:T(1,128)} %reshape.140), calls=%async_computation.3 | async-start | bytes 524288 | tf_op jit(solution)/shard_map/all_to_all | solution.py:146
  165.6 4.6 %copy.148 = f32[4,64,256]{0,2,1:T(8,128)} copy(f32[4,64,256]{2,1,0:T(8,128)S(1)} %get-tuple-element.36) | data formatting | bytes 524288 | tf_op jit(solution)/shard_map/reshape | solution.py:124
  170.3 74.5 %reduce = f32[16384,4]{1,0:T(8,128)} reduce(f32[16384,1,4]{2,1,0:T(1,128)} %bitcast.69, f32[]{:T(128)} %broadcast.144), dimensions={1}, to_apply=%bitcast.61.reduce_sub_computation | reduce | bytes 524292
  244.8 9.1 %reshape.138 = f32[32,1,2048]{2,1,0:T(1,128)} reshape(f32[16384,4]{1,0:T(8,128)} %reduce) | data formatting | bytes 524288
  253.9 8.4 %all-to-all-start.2 = ((f32[32,1,2048]{2,1,0:T(1,128)}), f32[32,1,2048]{2,1,0:T(1,128)S(1)}, u32[]{:S(2)}, u32[]{:S(2)}) async-start(f32[32,1,2048]{2,1,0:T(1,128)} %reshape.138), calls=%async_computation.2 | async-start | bytes 524288 | tf_op jit(solution)/shard_map/all_to_all | solution.py:145
  263.3 1.3 reduce.3
  264.5 14.7 %reshape.141 = f32[16384,1,4]{2,1,0:T(1,128)} reshape(f32[32,2048]{1,0:T(8,128)S(1)} %reduce.3) | data formatting | bytes 524288
  279.3 5.3 %copy.150 = f32[1,4,32,512]{3,2,1,0:T(8,128)S(1)} copy(f32[1,4,32,512]{1,3,2,0:T(8,128)} %bitcast.70) | data formatting | bytes 524288 | tf_op jit(solution)/shard_map/all_to_all | solution.py:146
  285.3 2.1 collective-permute-start.1
  288.5 1.3 reduce.1
  289.7 14.7 %reshape.139 = f32[16384,1,4]{2,1,0:T(1,128)} reshape(f32[32,2048]{1,0:T(8,128)S(1)} %reduce.1) | data formatting | bytes 524288
  304.5 5.3 %copy.132 = f32[1,32,4,512]{3,2,1,0:T(4,128)S(1)} copy(f32[1,32,4,512]{2,3,1,0:T(8,128)} %bitcast.71) | data formatting | bytes 524288 | tf_op jit(solution)/shard_map/all_to_all | solution.py:145
  313.2 1.7 copy.165
  (61 shorter events, 11.8 us)
Async XLA Ops:
  7.2 20.2 %copy-start.4 = (pred[8,65]{0,1:T(8,128)(4,1)S(1)}, pred[8,65]{0,1:T(8,128)(4,1)}, u32[]{:S(2)}) copy-start(pred[8,65]{0,1:T(8,128)(4,1)} %constant.74) | copy-start | bytes 1564
  8.1 17.6 %collective-permute-start = (f32[1,128,3]{2,1,0:T(8,128)S(1)}, f32[1,128,3]{2,1,0:T(8,128)S(1)}, u32[]{:S(2)}, u32[]{:S(2)}) collective-permute-start(f32[1,128,3]{2,1,0:T(8,128)S(1)} %slice.64), channel_id=1, source_target_pairs={{0,8},{8,16},{16,24},{24,32},{32,40},{40,48},{48,56},{56,64},{64,7... | collective-permute-start | bytes 4616 | tf_op jit(solution)/shard_map/ppermute | solution.py:14
  15.1 20.4 %all-to-all-start.1 = ((f32[1,128,512]{2,0,1:T(1,128)}), f32[1,128,512]{2,0,1:T(1,128)S(1)}, u32[]{:S(2)}, u32[]{:S(2)}) async-start(f32[1,128,512]{2,0,1:T(1,128)} %copy.125), calls=%async_computation.1 | async-start | bytes 524288 | tf_op jit(solution)/shard_map/all_to_all | solution.py:141
  25.8 15.5 %copy-start.2 = (f32[4,16384]{1,0:T(4,128)S(1)}, f32[4,16384]{1,0:T(4,128)}, u32[]{:S(2)}) copy-start(f32[4,16384]{1,0:T(4,128)} %param.10) | copy-start | bytes 786436
  35.5 17.3 %all-to-all-start = ((f32[1,128,512]{2,0,1:T(1,128)}), f32[1,128,512]{2,0,1:T(1,128)S(1)}, u32[]{:S(2)}, u32[]{:S(2)}) async-start(f32[1,128,512]{2,0,1:T(1,128)} %copy.123), calls=%async_computation | async-start | bytes 524288 | tf_op jit(solution)/shard_map/all_to_all | solution.py:140
  160.5 93.3 %all-to-all-start.3 = ((f32[32,1,2048]{2,1,0:T(1,128)}), f32[32,1,2048]{2,1,0:T(1,128)S(1)}, u32[]{:S(2)}, u32[]{:S(2)}) async-start(f32[32,1,2048]{2,1,0:T(1,128)} %reshape.140), calls=%async_computation.3 | async-start | bytes 524288 | tf_op jit(solution)/shard_map/all_to_all | solution.py:146
  253.9 34.6 %all-to-all-start.2 = ((f32[32,1,2048]{2,1,0:T(1,128)}), f32[32,1,2048]{2,1,0:T(1,128)S(1)}, u32[]{:S(2)}, u32[]{:S(2)}) async-start(f32[32,1,2048]{2,1,0:T(1,128)} %reshape.138), calls=%async_computation.2 | async-start | bytes 524288 | tf_op jit(solution)/shard_map/all_to_all | solution.py:145
  262.3 50.9 %all-reduce.2.cloned.1.call-start = ((), (), s32[]{:S(2)}) async-start(), calls=%async_computation.4 | async-start | bytes 524288 | tf_op jit(solution)/shard_map/psum | solution.py:148
  279.3 5.6 %copy-start.1 = (f32[1,128,512]{2,1,0:T(8,128)S(1)}, f32[1,128,512]{2,1,0:T(8,128)}, u32[]{:S(2)}) copy-start(f32[1,128,512]{2,1,0:T(8,128)} %param.9) | copy-start | bytes 786436
  285.3 25.4 %collective-permute-start.1 = (f32[1,128,3]{2,0,1:T(1,128)S(1)}, f32[1,128,3]{2,0,1:T(1,128)S(1)}, u32[]{:S(2)}, u32[]{:S(2)}) collective-permute-start(f32[1,128,3]{2,0,1:T(1,128)S(1)} %slice.101), channel_id=1, source_target_pairs={{8,0},{16,8},{24,16},{32,24},{40,32},{48,40},{56,48},{64,56},{72,6... | collective-permute-start | bytes 4616 | tf_op jit(solution)/shard_map/ppermute | solution.py:14
  304.5 5.5 %copy-start = (f32[1,128,512]{2,1,0:T(8,128)S(1)}, f32[1,128,512]{2,1,0:T(8,128)}, u32[]{:S(2)}) copy-start(f32[1,128,512]{2,1,0:T(8,128)} %param.6) | copy-start | bytes 786436
  309.8 2.2 copy-start.3
Sparse Core Ops, SparseCore 0:
  265.7 36.7 all-reduce.1
where the time goes:
time: 326 us; the launch traced here: 322 us
  other arithmetic  160 us (49%)
  local copies, waits for them, and re-layouts  79.4 us (24%)
  starting transfers between devices  35.1 us (11%)
  matrix products  17 us (5%)
  waiting for transfers between devices  15.6 us (5%)
  between operations  14.7 us (5%)
    unnamed x2, other arithmetic  149 us
    unnamed x24, local copies, waits for them, and re-layouts  54.6 us
    all_to_all x1, starting transfers between devices, shards(): lax.all_to_all(grad_conv, 'ctx', split_axis=1, concat_axis=2, tiled=True)  8.85 us
    all_to_all x1, waiting for transfers between devices, shards(): lax.all_to_all(gated, 'ctx', split_axis=1, concat_axis=2, tiled=True)  8.53 us
    all_to_all x1, starting transfers between devices, shards(): lax.all_to_all(conv_own, 'ctx', split_axis=2, concat_axis=1, tiled=True)  8.42 us
    ppermute x2, starting transfers between devices, from_behind(): return lax.ppermute(block, axis, route)  7.05 us
    all_to_all x1, waiting for transfers between devices, shards(): lax.all_to_all(grad_conv, 'ctx', split_axis=1, concat_axis=2, tiled=True)  7 us
  transfers between devices with their start and end apart: 7, of which 2 were waited for; matrix products, arithmetic and copies ran while one was open for 45% of the time, Pallas kernels for 0%

commit v1 on v0

v1 whole, which is shorter than its diff:
```python
import functools
import math

import jax
import jax.numpy as jnp
import numpy as np
from jax import lax
from jax.experimental import pallas as pl
from jax.experimental.pallas import tpu as pltpu
from jax.sharding import PartitionSpec as P

LANES = 128
F32 = jnp.float32
BF16 = jnp.bfloat16


def halves(table):
    high = table.astype(np.float32).astype(jnp.bfloat16)
    low = (table - high.astype(np.float64)).astype(np.float32).astype(jnp.bfloat16)
    return high, low


def make_tables(rows, cols):
    length = rows * cols
    shifted = np.arange(rows) + 0.25
    turn_one = 2 * np.pi * np.outer(shifted, np.arange(rows)) / rows
    turn_mid = 2 * np.pi * np.outer(shifted, np.arange(cols)) / length
    turn_two = 2 * np.pi * np.outer(np.arange(cols), np.arange(cols)) / cols
    cos, sin = np.cos(turn_two), np.sin(turn_two)
    first = np.concatenate([np.cos(turn_one), -np.sin(turn_one)], 0)
    second = np.block([[cos, -sin], [sin, cos]])
    second_inv = np.block([[cos, sin], [-sin, cos]])
    scale = length**-1.5
    first_inv = np.concatenate([np.cos(turn_one).T, -np.sin(turn_one).T], 1) * scale
    left = lambda m: np.concatenate([halves(m)[0], halves(m)[0], halves(m)[1]], 1)
    right = lambda m: np.concatenate([halves(m)[0], halves(m)[0], halves(m)[1]], 0)
    mid = np.concatenate([np.cos(turn_mid), -np.sin(turn_mid)], 1).astype(np.float32)
    return left(first), right(second), right(second_inv), left(first_inv), mid


def cut(x):
    high = x.astype(BF16)
    return high, (x - high.astype(F32)).astype(BF16)


def dot(a, b):
    return jnp.dot(a, b, preferred_element_type=F32)


def lane_ids(shape):
    return lax.broadcasted_iota(jnp.int32, shape, len(shape) - 1)


def row_ids(shape):
    return lax.broadcasted_iota(jnp.int32, shape, 0)


def put_cut(lhs, row, re, im):
    n = re.shape[0]
    re_hi, re_lo = cut(re)
    im_hi, im_lo = cut(im)
    for place, piece in enumerate((re_hi, im_hi, re_lo, im_lo, re_hi, im_hi)):
        lhs[pl.ds(row, n), pl.ds(place * LANES, LANES)] = piece


def forward(signals, first, second, mid, lhs, row):
    rows = signals[0].shape[0]
    turn_re = mid[:, :LANES]
    turn_im = mid[:, LANES:]
    for pair in range(0, len(signals), 2):
        hi, lo = cut(jnp.concatenate(signals[pair : pair + 2], 1))
        part = dot(first[...], jnp.concatenate([hi, lo, hi], 0))
        for which in range(2):
            re = part[:rows, which * LANES : (which + 1) * LANES]
            im = part[rows:, which * LANES : (which + 1) * LANES]
            put_cut(
                lhs,
                row + (pair + which) * rows,
                re * turn_re - im * turn_im,
                re * turn_im + im * turn_re,
            )
    return dot(lhs[pl.ds(row, len(signals) * rows), :], second[...])


def backward(count, rows, second_inv, first_inv, mid, lhs, row):
    turn_re = mid[:, :LANES]
    turn_im = mid[:, LANES:]
    back = dot(lhs[pl.ds(row, count * rows), :], second_inv[...])
    pairs = []
    for pair in range(0, count, 2):
        columns = []
        for which in range(2):
            here = back[(pair + which) * rows : (pair + which + 1) * rows]
            re, im = here[:, :LANES], here[:, LANES:]
            columns.append(
                jnp.concatenate([re * turn_re + im * turn_im, im * turn_re - re * turn_im], 0)
            )
        hi, lo = cut(jnp.concatenate(columns, 1))
        out = dot(first_inv[...], jnp.concatenate([hi, lo, hi], 0))
        pairs += [out[:, :LANES], out[:, LANES:]]
    return pairs


def short_taps(keys, taps):
    lane = lane_ids(keys.shape)
    once = jnp.where(lane < 1, 0.0, pltpu.roll(keys, 1, 1))
    twice = jnp.where(lane < 2, 0.0, pltpu.roll(keys, 2, 1))
    return taps[:, 0:1] * keys + taps[:, 1:2] * once + taps[:, 2:3] * twice


def pack_body(own, blocks, grad_out, query, keys, values, taps, out, scratch):
    width = 2 * own + 1
    chunk = width * blocks
    key, value, tap = keys[0], values[0], taps[...]
    chans, span = key.shape
    peers = chans // own
    gated = short_taps(key, tap) * value
    grad = grad_out[0] * query[0]
    lane = lane_ids((chans, LANES))
    tail = key[:, span - LANES :]
    after = tap[:, 2:3] * pltpu.roll(tail, 2, 1) + jnp.where(
        lane < 1, tap[:, 1:2] * pltpu.roll(tail, 1, 1), 0.0
    )
    head = jnp.where(lane < 4, pltpu.roll(value[:, :LANES], 2, 1), 0.0)
    out[pl.ds(2 * own, chans, stride=width), :] = jnp.where(lane < 2, after, head)
    for t, whole in enumerate((gated, grad)):
        for j in range(blocks):
            scratch[t, j] = whole[:, j * LANES : (j + 1) * LANES]
    for t in range(2):
        for j in range(blocks):
            for c in range(own):
                out[pl.ds(width * j + own * t + c, peers, stride=chunk), :] = scratch[
                    t, j, pl.ds(c, peers, stride=own), :
                ]


def filter_body(long_filter, first, second, mid, spec, scratch, lhs):
    own, length = long_filter.shape
    rows = length // LANES
    for n in range(rows):
        scratch[pl.ds(own * n, own), :] = long_filter[:, pl.ds(n * LANES, LANES)]
    signals = [scratch[pl.ds(c, rows, stride=own), :] for c in range(own)]
    spec[...] = forward(signals, first, second, mid, lhs, 0)


def main_body(
    own, blocks, recv, filt, first, second, second_inv, first_inv, mid, out, cross, edge, tile, lhs
):
    width = 2 * own + 1
    rows = recv.shape[0] // width
    peers = rows // blocks
    ext = recv[pl.ds(2 * own, rows, stride=width), :]
    lane, line = lane_ids(ext.shape), row_ids(ext.shape)
    heads = pltpu.roll(ext, LANES - 2, 1)
    before = jnp.where(line < own, 0.0, pltpu.roll(ext, own, 0))
    edge[...] = jnp.where(lane < 2, heads * before, 0.0)
    for c in range(own):
        tile[c] = recv[pl.ds(c, rows, stride=width), :]
        tile[c, pl.ds(0, peers, stride=blocks), :] += edge[pl.ds(c, peers, stride=own), :]
    gate = forward([tile[c] for c in range(own)], first, second, mid, lhs, 0)
    grads = [recv[pl.ds(own + c, rows, stride=width), :] for c in range(own)]
    grad = forward(grads, first, second, mid, lhs, own * rows)
    for c in range(own):
        here = slice(c * rows, (c + 1) * rows)
        g_re, g_im = gate[here, :LANES], gate[here, LANES:]
        d_re, d_im = grad[here, :LANES], grad[here, LANES:]
        f_re, f_im = filt[here, :LANES], filt[here, LANES:]
        put_cut(lhs, c * rows, g_re * f_re - g_im * f_im, g_re * f_im + g_im * f_re)
        put_cut(lhs, (own + c) * rows, d_re * f_re + d_im * f_im, d_im * f_re - d_re * f_im)
        cross[here, :LANES] = d_re * g_re + d_im * g_im
        cross[here, LANES:] = d_im * g_re - d_re * g_im
    signals = backward(2 * own, rows, second_inv, first_inv, mid, lhs, 0)
    for q, signal in enumerate(signals):
        out[pl.ds(q, rows, stride=width), :] = signal
    for c in range(own):
        tile[c] = signals[own + c]
        edge[pl.ds(c, peers, stride=own), :] = tile[c, pl.ds(0, peers, stride=blocks), :]
    behind = jnp.where(line < rows - own, pltpu.roll(edge[...] * heads, rows - own, 0), 0.0)
    shifted = jnp.where(lane < 4, pltpu.roll(before, 2, 1), 0.0)
    out[pl.ds(2 * own, rows, stride=width), :] = jnp.where(lane < 2, behind, shifted)


def cross_body(cross, second_inv, first_inv, mid, part, scratch, lhs):
    own, length = part.shape
    rows = length // LANES
    for c in range(own):
        here = slice(c * rows, (c + 1) * rows)
        put_cut(lhs, c * rows, cross[here, :LANES], cross[here, LANES:])
    for c, signal in enumerate(backward(own, rows, second_inv, first_inv, mid, lhs, 0)):
        scratch[pl.ds(c, rows, stride=own), :] = signal
    for n in range(rows):
        part[:, pl.ds(n * LANES, LANES)] = scratch[pl.ds(own * n, own), :]


def finish_body(
    own, blocks, recv, grad_out, keys, values, taps, grad_query, grad_keys, grad_values, scratch
):
    width = 2 * own + 1
    chunk = width * blocks
    key, value, tap = keys[0], values[0], taps[...]
    chans, span = key.shape
    peers = chans // own
    for t in range(2):
        for j in range(blocks):
            for c in range(own):
                scratch[t, j, pl.ds(c, peers, stride=own), :] = recv[
                    pl.ds(width * j + own * t + c, peers, stride=chunk), :
                ]
    conv = jnp.concatenate([scratch[0, j] for j in range(blocks)], 1)
    grad = jnp.concatenate([scratch[1, j] for j in range(blocks)], 1)
    ext = recv[pl.ds(2 * own, chans, stride=width), :]
    lane = lane_ids((chans, LANES))
    turned = pltpu.roll(ext, LANES - 2, 1)
    grad_query[0] = grad_out[0] * conv
    short = short_taps(key, tap)
    fixed = short[:, :LANES] + jnp.where(lane < 2, turned, 0.0)
    short = jnp.concatenate([fixed, short[:, LANES:]], 1)
    grad_values[0] = grad * short
    part = grad * value
    once = pltpu.roll(part, span - 1, 1)
    twice = pltpu.roll(part, span - 2, 1)
    last = span - LANES
    once_end = jnp.where(lane < LANES - 1, once[:, last:], pltpu.roll(ext, LANES - 1, 1))
    twice_end = jnp.where(lane < LANES - 2, twice[:, last:], turned)
    once = jnp.concatenate([once[:, :last], once_end], 1)
    twice = jnp.concatenate([twice[:, :last], twice_end], 1)
    grad_keys[0] = tap[:, 0:1] * part + tap[:, 1:2] * once + tap[:, 2:3] * twice


def call(body, name, outs, scratch, args, flops):
    moved = sum(a.size * a.dtype.itemsize for a in args) + sum(
        math.prod(o.shape) * o.dtype.itemsize for o in outs
    )
    return pl.pallas_call(
        body,
        out_shape=outs,
        scratch_shapes=scratch,
        name=name,
        cost_estimate=pl.CostEstimate(flops=flops, bytes_accessed=moved, transcendentals=0),
        compiler_params=pltpu.CompilerParams(vmem_limit_bytes=32 * 2**20),
    )(*args)


def shape(*dims):
    return jax.ShapeDtypeStruct(dims, F32)


def exchange(x, parts):
    rows = x.shape[0] // parts
    assert rows % 4 == 0
    moved = x.reshape(parts, rows // 4, 4, LANES)
    moved = lax.all_to_all(moved, "ctx", split_axis=0, concat_axis=0, tiled=True)
    return moved.reshape(x.shape)


def shards(grad_out, query, keys, values, long_filter, short_filter):
    _, chans, span = keys.shape
    own, length = long_filter.shape
    parts = length // span
    blocks = span // LANES
    rows = length // LANES
    assert chans == own * parts and rows == LANES and blocks == own
    packed_rows = parts * blocks * (2 * own + 1)
    tables = make_tables(rows, LANES)
    first, second, second_inv, first_inv, mid = (jnp.asarray(t) for t in tables)
    wide = 6 * LANES
    work = 6 * own * rows * wide * 2 * LANES
    tiles = pltpu.VMEM((2, blocks, chans, LANES), F32)
    packed = call(
        functools.partial(pack_body, own, blocks),
        "pack",
        (shape(packed_rows, LANES),),
        [tiles],
        (grad_out, query, keys, values, short_filter),
        10 * chans * span,
    )[0]
    received = exchange(packed, parts)
    spec = call(
        filter_body,
        "filter_spectrum",
        (shape(own * rows, 2 * LANES),),
        [pltpu.VMEM((own * rows, LANES), F32), pltpu.VMEM((own * rows, wide), BF16)],
        (long_filter, first, second, mid),
        work,
    )[0]
    sent, cross = call(
        functools.partial(main_body, own, blocks),
        "main",
        (shape(packed_rows, LANES), shape(own * rows, 2 * LANES)),
        [
            pltpu.VMEM((rows, LANES), F32),
            pltpu.VMEM((own, rows, LANES), F32),
            pltpu.VMEM((2 * own * rows, wide), BF16),
        ],
        (received, spec, first, second, second_inv, first_inv, mid),
        4 * work,
    )
    returned = exchange(sent, parts)
    part = call(
        cross_body,
        "cross",
        (shape(own, length),),
        [pltpu.VMEM((own * rows, LANES), F32), pltpu.VMEM((own * rows, wide), BF16)],
        (cross, second_inv, first_inv, mid),
        work,
    )[0]
    grad_long = part + lax.ppermute(part, "seq", [(0, 1), (1, 0)])
    grad_query, grad_keys, grad_values = call(
        functools.partial(finish_body, own, blocks),
        "finish",
        (shape(*keys.shape),) * 3,
        [tiles],
        (returned, grad_out, keys, values, short_filter),
        10 * chans * span,
    )
    return grad_query, grad_keys, grad_values, grad_long


def solution(mesh):
    block = P("seq", "ch", "ctx")
    rows = P(("ch", "ctx"), None)
    return jax.shard_map(
        shards,
        mesh=mesh,
        in_specs=(block, block, block, block, rows, P("ch", None)),
        out_specs=(block, block, block, rows),
        check_vma=False,
    )
```

time: 326 us -> 64.6 us (0.20)
  other arithmetic: 160 us -> 0.77 us
  local copies, waits for them, and re-layouts: 79.4 us -> 4.63 us
  matrix products: 17 us -> 0 us
  starting transfers between devices: 35.1 us -> 19.6 us
  waiting for transfers between devices: 15.6 us -> 30.5 us
  between operations: 14.7 us -> 0.75 us
  Pallas kernels: 0 us -> 7.34 us
    unnamed x2 -> x0, other arithmetic: 149 us -> none
    unnamed x24 -> x27, local copies, waits for them, and re-layouts: 54.6 us -> 4.63 us
    dot_general x4 -> x0, matrix products: 16.8 us -> none  [the longest x1 5.69 us: inverse(): jnp.dot(joined.reshape(outer_len * row_count, 2 * inner_len), inner_inv,...]
    all_to_all x7 -> x0, local copies, waits for them, and re-layouts: 11.3 us -> none  [the longest x3 5.7 us: shards(): lax.all_to_all(grad_gated_own, 'ctx', split_axis=2, concat_axis=1, tiled=...]
    all_to_all x4 -> x2, starting transfers between devices: 28 us -> 16.9 us  [exchange(): lax.all_to_all(moved, 'ctx', split_axis=0, concat_axis=0, tiled=True)]
    ppermute x2 -> x1, waiting for transfers between devices: 0.01 us -> 9.46 us  [shards(): grad_long = part + lax.ppermute(part, 'seq', [(0, 1), (1, 0)])]
    reshape x2 -> x0, local copies, waits for them, and re-layouts: 9.27 us -> none  [the longest x1 4.64 us: long_terms(): grad_gated_own = signals[many:2 * many].reshape(seq_here, own_chans, length)]
    pallas_call x0 -> x5, Pallas kernels: none -> 7.34 us  [call(): pl.pallas_call(body, out_shape=outs, scratch_shapes=scratch, name=name, c...]
  transfers between devices with their start and end apart: 7 -> 3, of which waited for: 2 -> 3; matrix products, arithmetic and copies ran while one was open for 45% -> 1% of each run, Pallas kernels for 0% -> 2%
where the time goes in v1:
time: 64.6 us; the launch traced here: 63.6 us
  waiting for transfers between devices  30.5 us (47%)
  starting transfers between devices  19.6 us (30%)
  Pallas kernels  7.34 us (11%)
  local copies, waits for them, and re-layouts  4.63 us (7%)
  other arithmetic  0.77 us (1%)
  between operations  0.75 us (1%)
    all_to_all x2, waiting for transfers between devices, exchange(): lax.all_to_all(moved, 'ctx', split_axis=0, concat_axis=0, tiled=True)  21 us
    all_to_all x2, starting transfers between devices, exchange(): lax.all_to_all(moved, 'ctx', split_axis=0, concat_axis=0, tiled=True)  16.9 us
    ppermute x1, waiting for transfers between devices, shards(): grad_long = part + lax.ppermute(part, 'seq', [(0, 1), (1, 0)])  9.46 us
    pallas_call x5, Pallas kernels, call(): pl.pallas_call(body, out_shape=outs, scratch_shapes=scratch, name=name, c...  7.34 us
    unnamed x27, local copies, waits for them, and re-layouts  4.63 us
    ppermute x1, starting transfers between devices, shards(): grad_long = part + lax.ppermute(part, 'seq', [(0, 1), (1, 0)])  2.71 us
  transfers between devices with their start and end apart: 3, of which 3 were waited for; matrix products, arithmetic and copies ran while one was open for 1% of the time, Pallas kernels for 2%

profile of v1, /device:TPU:1, one launch (start us, length us, event | category | flops | bytes accessed | tf_op | source)
XLA Modules:
  0.0 63.6 jit_solution(3197228643095491184)
XLA Ops:
  0.6 0.8 %copy.15.taps = f32[128,3]{1,0:T(8,128)S(1)} copy(f32[128,3]{0,1:T(4,128)} %param.16) | data formatting | bytes 3072 | tf_op args[5]
  1.4 0.0 copy-start
  1.4 0.9 %copy-done = f32[1,128,512]{2,1,0:T(8,128)S(1)} copy-done((f32[1,128,512]{2,1,0:T(8,128)S(1)}, f32[1,128,512]{2,1,0:T(8,128)}, u32[]{:S(2)}) %copy-start) | copy-done | bytes 262168
  2.4 0.9 %copy-done.2 = f32[1,128,512]{2,1,0:T(8,128)S(1)} copy-done((f32[1,128,512]{2,1,0:T(8,128)S(1)}, f32[1,128,512]{2,1,0:T(8,128)}, u32[]{:S(2)}) %copy-start.2) | copy-done | bytes 262168
  3.3 0.9 %copy-done.4 = f32[1,128,512]{2,1,0:T(8,128)S(1)} copy-done((f32[1,128,512]{2,1,0:T(8,128)S(1)}, f32[1,128,512]{2,1,0:T(8,128)}, u32[]{:S(2)}) %copy-start.4) | copy-done | bytes 262168
  4.3 0.9 %copy-done.6 = f32[1,128,512]{2,1,0:T(8,128)S(1)} copy-done((f32[1,128,512]{2,1,0:T(8,128)S(1)}, f32[1,128,512]{2,1,0:T(8,128)}, u32[]{:S(2)}) %copy-start.6) | copy-done | bytes 262168
  5.2 1.2 %pack.1 = f32[1152,128]{1,0:T(8,128)} custom-call(f32[1,128,512]{2,1,0:T(8,128)S(1)} %copy-done, f32[1,128,512]{2,1,0:T(8,128)S(1)} %copy-done.6, f32[1,128,512]{2,1,0:T(8,128)S(1)} %copy-done.2, f32[1,128,512]{2,1,0:T(8,128)S(1)} %copy-done.4, f32[128,3]{1,0:T(8,128)S(1)} %copy.15.taps), custom_call_target="tpu_custom_call" | custom-call | flops 655360 | bytes 1639936 | tf_op jit(solution)/shard_map/pack/pallas_call | solution.py:234
  6.4 11.3 %all-to-all-start = ((f32[32,9,4,128]{3,2,1,0:T(4,128)}), f32[32,9,4,128]{3,2,1,0:T(4,128)S(1)}, u32[]{:S(2)}, u32[]{:S(2)}) async-start(f32[32,9,4,128]{3,2,1,0:T(4,128)} %bitcast), calls=%async_computation | async-start | bytes 1179648 | tf_op jit(solution)/shard_map/all_to_all | solution.py:252
  17.7 0.0 copy-done.7
  17.7 0.0 copy-done.9
  17.7 0.0 copy-done.11
  17.7 0.0 copy-done.12
  17.7 0.0 copy-start.8
  17.7 0.0 copy-start.10
  17.8 0.7 %filter_spectrum.1.filt = f32[512,256]{1,0:T(8,128)S(1)} custom-call(f32[4,16384]{1,0:T(4,128)S(1)} %copy-done.7, bf16[256,384]{1,0:T(8,128)(2,1)S(1)} %copy-done.11, bf16[768,256]{1,0:T(8,128)(2,1)S(1)} %copy-done.9, f32[128,256]{1,0:T(8,128)S(1)} %copy-done.12), custom_call_target="tpu_custom_call" | custom-call | flops 603979776 | bytes 1507328 | tf_op jit(solution)/shard_map/filter_spectrum/pallas_call | solution.py:234
  18.5 16.9 %all-to-all-done = f32[32,9,4,128]{3,2,1,0:T(4,128)S(1)} async-done(((f32[32,9,4,128]{3,2,1,0:T(4,128)}), f32[32,9,4,128]{3,2,1,0:T(4,128)S(1)}, u32[]{:S(2)}, u32[]{:S(2)}) %all-to-all-start) | async-done | bytes 589856 | tf_op jit(solution)/shard_map/all_to_all | solution.py:252
  35.4 0.0 copy-done.8
  35.4 0.0 copy-done.10
  35.4 3.3 %main.1 = (f32[1152,128]{1,0:T(8,128)}, f32[512,256]{1,0:T(8,128)S(1)}) custom-call(f32[1152,128]{1,0:T(8,128)S(1)} %bitcast.5, f32[512,256]{1,0:T(8,128)S(1)} %filter_spectrum.1.filt, bf16[256,384]{1,0:T(8,128)(2,1)S(1)} %copy-done.11, bf16[768,256]{1,0:T(8,128)(2,1)S(1)} %copy-done.9, bf16[768,256]{1,0:T(8,128)(2,1)S(1)} %copy-done.8, ...), custom_call_target="tpu_custom_call" | custom-call | flops 2415919104 | bytes 3538944 | tf_op jit(solution)/shard_map/main/pallas_call | solution.py:234
  38.7 5.6 %all-to-all-start.1 = ((f32[32,9,4,128]{3,2,1,0:T(4,128)}), f32[32,9,4,128]{3,2,1,0:T(4,128)S(1)}, u32[]{:S(2)}, u32[]{:S(2)}) async-start(f32[32,9,4,128]{3,2,1,0:T(4,128)} %bitcast.2), calls=%async_computation.1 | async-start | bytes 1179648 | tf_op jit(solution)/shard_map/all_to_all | solution.py:252
  44.3 0.8 %cross.1 = f32[4,16384]{1,0:T(4,128)S(1)} custom-call(f32[512,256]{1,0:T(8,128)S(1)} %get-tuple-element.13.cross, bf16[768,256]{1,0:T(8,128)(2,1)S(1)} %copy-done.8, bf16[128,768]{1,0:T(8,128)(2,1)S(1)} %copy-done.10, f32[128,256]{1,0:T(8,128)S(1)} %copy-done.12), custom_call_target="tpu_custom_call" | custom-call | flops 603979776 | bytes 1507328 | tf_op jit(solution)/shard_map/cross/pallas_call | solution.py:234
  45.1 0.0 copy-start.1
  45.1 0.0 copy-start.3
  45.1 0.0 copy-start.5
  45.1 2.7 %collective-permute-start = (f32[4,16384]{1,0:T(4,128)S(1)}, f32[4,16384]{1,0:T(4,128)S(1)}, u32[]{:S(2)}, u32[]{:S(2)}) collective-permute-start(f32[4,16384]{1,0:T(4,128)S(1)} %cross.1), channel_id=1, source_target_pairs={{0,4},{4,0},{1,5},{5,1},{2,6},{6,2},{3,7},{7,3},{8,12},{12,8},{9,1... | collective-permute-start | bytes 786440 | tf_op jit(solution)/shard_map/ppermute | solution.py:307
  47.9 9.5 %collective-permute-done = f32[4,16384]{1,0:T(4,128)S(1)} collective-permute-done((f32[4,16384]{1,0:T(4,128)S(1)}, f32[4,16384]{1,0:T(4,128)S(1)}, u32[]{:S(2)}, u32[]{:S(2)}) %collective-permute-start) | collective-permute-done | bytes 262176 | tf_op jit(solution)/shard_map/ppermute | solution.py:307
  57.3 0.8 %add.3 = f32[4,16384]{1,0:T(4,128)} add(f32[4,16384]{1,0:T(4,128)S(1)} %cross.1, f32[4,16384]{1,0:T(4,128)S(1)} %collective-permute-done) | non-fusion elementwise | flops 65536 | bytes 786432 | tf_op jit(solution)/shard_map/add | solution.py:307
  58.1 4.1 %all-to-all-done.1 = f32[32,9,4,128]{3,2,1,0:T(4,128)S(1)} async-done(((f32[32,9,4,128]{3,2,1,0:T(4,128)}), f32[32,9,4,128]{3,2,1,0:T(4,128)S(1)}, u32[]{:S(2)}, u32[]{:S(2)}) %all-to-all-start.1) | async-done | bytes 589856 | tf_op jit(solution)/shard_map/all_to_all | solution.py:252
  62.2 0.0 copy-done.1
  62.2 0.0 copy-done.3
  62.2 0.0 copy-done.5
  62.2 1.4 %finish.1 = (f32[1,128,512]{2,1,0:T(8,128)}, f32[1,128,512]{2,1,0:T(8,128)}, f32[1,128,512]{2,1,0:T(8,128)}) custom-call(f32[1152,128]{1,0:T(8,128)S(1)} %bitcast.4, f32[1,128,512]{2,1,0:T(8,128)S(1)} %copy-done.1, f32[1,128,512]{2,1,0:T(8,128)S(1)} %copy-done.3, f32[1,128,512]{2,1,0:T(8,128)S(1)} %copy-done.5, f32[128,3]{1,0:T(8,128)S(1)} %copy.15.taps), custom_call_target="tpu_custom_call" | custom-call | flops 655360 | bytes 2164224 | tf_op jit(solution)/shard_map/finish/pallas_call | solution.py:234
  (7 shorter events, 0.0 us)
Async XLA Ops:
  1.4 0.9 %copy-start = (f32[1,128,512]{2,1,0:T(8,128)S(1)}, f32[1,128,512]{2,1,0:T(8,128)}, u32[]{:S(2)}) copy-start(f32[1,128,512]{2,1,0:T(8,128)} %grad_out.3) | copy-start | bytes 786436
  2.4 0.9 %copy-start.2 = (f32[1,128,512]{2,1,0:T(8,128)S(1)}, f32[1,128,512]{2,1,0:T(8,128)}, u32[]{:S(2)}) copy-start(f32[1,128,512]{2,1,0:T(8,128)} %keys.3) | copy-start | bytes 786436
  3.3 0.9 %copy-start.4 = (f32[1,128,512]{2,1,0:T(8,128)S(1)}, f32[1,128,512]{2,1,0:T(8,128)}, u32[]{:S(2)}) copy-start(f32[1,128,512]{2,1,0:T(8,128)} %values.3) | copy-start | bytes 786436
  4.3 0.9 %copy-start.6 = (f32[1,128,512]{2,1,0:T(8,128)S(1)}, f32[1,128,512]{2,1,0:T(8,128)}, u32[]{:S(2)}) copy-start(f32[1,128,512]{2,1,0:T(8,128)} %query.1) | copy-start | bytes 786436
  6.4 11.3 %copy-start.7 = (f32[4,16384]{1,0:T(4,128)S(1)}, f32[4,16384]{1,0:T(4,128)}, u32[]{:S(2)}) copy-start(f32[4,16384]{1,0:T(4,128)} %long_filter.1) | copy-start | bytes 786436
  6.4 11.3 %copy-start.9 = (bf16[768,256]{1,0:T(8,128)(2,1)S(1)}, bf16[768,256]{1,0:T(8,128)(2,1)}, u32[]{:S(2)}) copy-start(bf16[768,256]{1,0:T(8,128)(2,1)} %constant.11.clone.second) | copy-start | bytes 1179652
  6.4 11.3 %copy-start.11 = (bf16[256,384]{1,0:T(8,128)(2,1)S(1)}, bf16[256,384]{1,0:T(8,128)(2,1)}, u32[]{:S(2)}) copy-start(bf16[256,384]{1,0:T(8,128)(2,1)} %constant.10.clone.first) | copy-start | bytes 589828
  6.4 11.3 %copy-start.12 = (f32[128,256]{1,0:T(8,128)S(1)}, f32[128,256]{1,0:T(8,128)}, u32[]{:S(2)}) copy-start(f32[128,256]{1,0:T(8,128)} %constant.14.clone.mid) | copy-start | bytes 393220
  6.4 29.0 %all-to-all-start = ((f32[32,9,4,128]{3,2,1,0:T(4,128)}), f32[32,9,4,128]{3,2,1,0:T(4,128)S(1)}, u32[]{:S(2)}, u32[]{:S(2)}) async-start(f32[32,9,4,128]{3,2,1,0:T(4,128)} %bitcast), calls=%async_computation | async-start | bytes 1179648 | tf_op jit(solution)/shard_map/all_to_all | solution.py:252
  17.7 17.7 %copy-start.8 = (bf16[768,256]{1,0:T(8,128)(2,1)S(1)}, bf16[768,256]{1,0:T(8,128)(2,1)}, u32[]{:S(2)}) copy-start(bf16[768,256]{1,0:T(8,128)(2,1)} %constant.12.clone.second_inv) | copy-start | bytes 1179652
  17.7 17.7 %copy-start.10 = (bf16[128,768]{1,0:T(8,128)(2,1)S(1)}, bf16[128,768]{1,0:T(8,128)(2,1)}, u32[]{:S(2)}) copy-start(bf16[128,768]{1,0:T(8,128)(2,1)} %constant.13.clone.first_inv) | copy-start | bytes 589828
  38.7 23.5 %all-to-all-start.1 = ((f32[32,9,4,128]{3,2,1,0:T(4,128)}), f32[32,9,4,128]{3,2,1,0:T(4,128)S(1)}, u32[]{:S(2)}, u32[]{:S(2)}) async-start(f32[32,9,4,128]{3,2,1,0:T(4,128)} %bitcast.2), calls=%async_computation.1 | async-start | bytes 1179648 | tf_op jit(solution)/shard_map/all_to_all | solution.py:252
  45.1 17.1 %copy-start.1 = (f32[1,128,512]{2,1,0:T(8,128)S(1)}, f32[1,128,512]{2,1,0:T(8,128)}, u32[]{:S(2)}) copy-start(f32[1,128,512]{2,1,0:T(8,128)} %grad_out.3) | copy-start | bytes 786436
  45.1 17.1 %copy-start.3 = (f32[1,128,512]{2,1,0:T(8,128)S(1)}, f32[1,128,512]{2,1,0:T(8,128)}, u32[]{:S(2)}) copy-start(f32[1,128,512]{2,1,0:T(8,128)} %keys.3) | copy-start | bytes 786436
  45.1 17.1 %copy-start.5 = (f32[1,128,512]{2,1,0:T(8,128)S(1)}, f32[1,128,512]{2,1,0:T(8,128)}, u32[]{:S(2)}) copy-start(f32[1,128,512]{2,1,0:T(8,128)} %values.3) | copy-start | bytes 786436
  45.1 12.2 %collective-permute-start = (f32[4,16384]{1,0:T(4,128)S(1)}, f32[4,16384]{1,0:T(4,128)S(1)}, u32[]{:S(2)}, u32[]{:S(2)}) collective-permute-start(f32[4,16384]{1,0:T(4,128)S(1)} %cross.1), channel_id=1, source_target_pairs={{0,4},{4,0},{1,5},{5,1},{2,6},{6,2},{3,7},{7,3},{8,12},{12,8},{9,1... | collective-permute-start | bytes 786440 | tf_op jit(solution)/shard_map/ppermute | solution.py:307

commit v2 on v1

--- a/solution.py
+++ b/solution.py
@@ -20,10 +20,14 @@
     return high, low
 
 
-def make_tables(rows, cols):
+def row_order(rows, blocks):
+    return np.arange(rows).reshape(-1, blocks).T.reshape(-1)
+
+
+def make_tables(rows, cols, order):
     length = rows * cols
     shifted = np.arange(rows) + 0.25
-    turn_one = 2 * np.pi * np.outer(shifted, np.arange(rows)) / rows
+    turn_one = 2 * np.pi * np.outer(shifted, order) / rows
     turn_mid = 2 * np.pi * np.outer(shifted, np.arange(cols)) / length
     turn_two = 2 * np.pi * np.outer(np.arange(cols), np.arange(cols)) / cols
     cos, sin = np.cos(turn_two), np.sin(turn_two)
@@ -101,64 +105,91 @@
     return pairs
 
 
+def tap_tiles(taps):
+    chans = taps.shape[1]
+    return [
+        jnp.transpose(jnp.broadcast_to(taps[j : j + 1, :], (LANES, chans)))
+        for j in range(taps.shape[0])
+    ]
+
+
 def short_taps(keys, taps):
     lane = lane_ids(keys.shape)
     once = jnp.where(lane < 1, 0.0, pltpu.roll(keys, 1, 1))
     twice = jnp.where(lane < 2, 0.0, pltpu.roll(keys, 2, 1))
-    return taps[:, 0:1] * keys + taps[:, 1:2] * once + taps[:, 2:3] * twice
-
-
-def pack_body(own, blocks, grad_out, query, keys, values, taps, out, scratch):
-    width = 2 * own + 1
-    chunk = width * blocks
-    key, value, tap = keys[0], values[0], taps[...]
-    chans, span = key.shape
+    wide = [jnp.concatenate([t] * (keys.shape[1] // LANES), 1) for t in taps]
+    return wide[0] * keys + wide[1] * once + wide[2] * twice
+
+
+def pack_body(
+    own, blocks, grad_out, query, keys, values, taps, out, held, scratch, edge, sems
+):
+    copies = [
+        pltpu.make_async_copy(source.at[0], held.at[i], sems.at[i])
+        for i, source in enumerate((keys, values, grad_out, query))
+    ]
+    for copy in copies:
+        copy.start()
+    chunk = 2 * own * blocks + 1
+    tap = tap_tiles(taps)
+    chans, span = keys.shape[1:]
     peers = chans // own
+    copies[0].wait()
+    copies[1].wait()
+    key, value = held[0], held[1]
     gated = short_taps(key, tap) * value
-    grad = grad_out[0] * query[0]
     lane = lane_ids((chans, LANES))
     tail = key[:, span - LANES :]
-    after = tap[:, 2:3] * pltpu.roll(tail, 2, 1) + jnp.where(
-        lane < 1, tap[:, 1:2] * pltpu.roll(tail, 1, 1), 0.0
+    after = tap[2] * pltpu.roll(tail, 2, 1) + jnp.where(
+        lane < 1, tap[1] * pltpu.roll(tail, 1, 1), 0.0
     )
     head = jnp.where(lane < 4, pltpu.roll(value[:, :LANES], 2, 1), 0.0)
-    out[pl.ds(2 * own, chans, stride=width), :] = jnp.where(lane < 2, after, head)
-    for t, whole in enumerate((gated, grad)):
+    edge[...] = jnp.where(lane < 2, after, head)
+    ends = edge[pl.ds(0, peers, stride=own), :]
+    for c in range(1, own):
+        ends = ends + pltpu.roll(edge[pl.ds(c, peers, stride=own), :], 4 * c, 1)
+    out[pl.ds(chunk - 1, peers, stride=chunk), :] = ends
+    for t in range(2):
+        if t == 1:
+            copies[2].wait()
+            copies[3].wait()
+            gated = held[2] * held[3]
         for j in range(blocks):
-            scratch[t, j] = whole[:, j * LANES : (j + 1) * LANES]
-    for t in range(2):
-        for j in range(blocks):
+            scratch[t, j] = gated[:, j * LANES : (j + 1) * LANES]
             for c in range(own):
-                out[pl.ds(width * j + own * t + c, peers, stride=chunk), :] = scratch[
+                out[pl.ds(2 * own * j + own * t + c, peers, stride=chunk), :] = scratch[
                     t, j, pl.ds(c, peers, stride=own), :
                 ]
 
 
-def filter_body(long_filter, first, second, mid, spec, scratch, lhs):
+def filter_body(order, long_filter, first, second, mid, spec, scratch, lhs):
     own, length = long_filter.shape
     rows = length // LANES
-    for n in range(rows):
-        scratch[pl.ds(own * n, own), :] = long_filter[:, pl.ds(n * LANES, LANES)]
+    for n, place in enumerate(order):
+        scratch[pl.ds(own * n, own), :] = long_filter[:, pl.ds(place * LANES, LANES)]
     signals = [scratch[pl.ds(c, rows, stride=own), :] for c in range(own)]
     spec[...] = forward(signals, first, second, mid, lhs, 0)
 
 
 def main_body(
-    own, blocks, recv, filt, first, second, second_inv, first_inv, mid, out, cross, edge, tile, lhs
+    own, blocks, recv, filt, first, second, second_inv, first_inv, mid, out, cross, lhs
 ):
-    width = 2 * own + 1
-    rows = recv.shape[0] // width
-    peers = rows // blocks
-    ext = recv[pl.ds(2 * own, rows, stride=width), :]
-    lane, line = lane_ids(ext.shape), row_ids(ext.shape)
-    heads = pltpu.roll(ext, LANES - 2, 1)
-    before = jnp.where(line < own, 0.0, pltpu.roll(ext, own, 0))
-    edge[...] = jnp.where(lane < 2, heads * before, 0.0)
-    for c in range(own):
-        tile[c] = recv[pl.ds(c, rows, stride=width), :]
-        tile[c, pl.ds(0, peers, stride=blocks), :] += edge[pl.ds(c, peers, stride=own), :]
-    gate = forward([tile[c] for c in range(own)], first, second, mid, lhs, 0)
-    grads = [recv[pl.ds(own + c, rows, stride=width), :] for c in range(own)]
+    chunk = 2 * own * blocks + 1
+    peers = recv.shape[0] // chunk
+    rows = peers * blocks
+    place = lambda t, j, c: pl.ds(2 * own * j + own * t + c, peers, stride=chunk)
+    ends = recv[pl.ds(chunk - 1, peers, stride=chunk), :]
+    lane, line = lane_ids(ends.shape), row_ids(ends.shape)
+    heads, before, gates, grads = [], [], [], []
+    for c in range(own):
+        heads.append(pltpu.roll(ends, (LANES - 4 * c - 2) % LANES, 1))
+        past = pltpu.roll(ends, (LANES - 4 * c) % LANES, 1) if c else ends
+        before.append(jnp.where(line < 1, 0.0, pltpu.roll(past, 1, 0)))
+        tiles = [recv[place(0, j, c), :] for j in range(blocks)]
+        tiles[0] = tiles[0] + jnp.where(lane < 2, heads[c] * before[c], 0.0)
+        gates.append(jnp.concatenate(tiles, 0))
+        grads.append(jnp.concatenate([recv[place(1, j, c), :] for j in range(blocks)], 0))
+    gate = forward(gates, first, second, mid, lhs, 0)
     grad = forward(grads, first, second, mid, lhs, own * rows)
     for c in range(own):
         here = slice(c * rows, (c + 1) * rows)
@@ -171,16 +202,19 @@
         cross[here, LANES:] = d_im * g_re - d_re * g_im
     signals = backward(2 * own, rows, second_inv, first_inv, mid, lhs, 0)
     for q, signal in enumerate(signals):
-        out[pl.ds(q, rows, stride=width), :] = signal
-    for c in range(own):
-        tile[c] = signals[own + c]
-        edge[pl.ds(c, peers, stride=own), :] = tile[c, pl.ds(0, peers, stride=blocks), :]
-    behind = jnp.where(line < rows - own, pltpu.roll(edge[...] * heads, rows - own, 0), 0.0)
-    shifted = jnp.where(lane < 4, pltpu.roll(before, 2, 1), 0.0)
-    out[pl.ds(2 * own, rows, stride=width), :] = jnp.where(lane < 2, behind, shifted)
-
-
-def cross_body(cross, second_inv, first_inv, mid, part, scratch, lhs):
+        for j in range(blocks):
+            out[place(q // own, j, q % own), :] = signal[j * peers : (j + 1) * peers]
+    ends = jnp.zeros(ends.shape, F32)
+    for c in range(own):
+        first_row = signals[own + c][:peers] * heads[c]
+        behind = jnp.where(line < peers - 1, pltpu.roll(first_row, peers - 1, 0), 0.0)
+        shifted = jnp.where(lane < 4, pltpu.roll(before[c], 2, 1), 0.0)
+        mine = jnp.where(lane < 2, behind, shifted)
+        ends = ends + (pltpu.roll(mine, 4 * c, 1) if c else mine)
+    out[pl.ds(chunk - 1, peers, stride=chunk), :] = ends
+
+
+def cross_body(order, cross, second_inv, first_inv, mid, part, scratch, lhs):
     own, length = part.shape
     rows = length // LANES
     for c in range(own):
@@ -188,27 +222,31 @@
         put_cut(lhs, c * rows, cross[here, :LANES], cross[here, LANES:])
     for c, signal in enumerate(backward(own, rows, second_inv, first_inv, mid, lhs, 0)):
         scratch[pl.ds(c, rows, stride=own), :] = signal
-    for n in range(rows):
-        part[:, pl.ds(n * LANES, LANES)] = scratch[pl.ds(own * n, own), :]
+    for n, place in enumerate(order):
+        part[:, pl.ds(place * LANES, LANES)] = scratch[pl.ds(own * n, own), :]
 
 
 def finish_body(
-    own, blocks, recv, grad_out, keys, values, taps, grad_query, grad_keys, grad_values, scratch
+    own, blocks, recv, grad_out, keys, values, taps, grad_query, grad_keys, grad_values, scratch, edge
 ):
-    width = 2 * own + 1
-    chunk = width * blocks
-    key, value, tap = keys[0], values[0], taps[...]
+    chunk = 2 * own * blocks + 1
+    key, value, tap = keys[0], values[0], tap_tiles(taps)
     chans, span = key.shape
     peers = chans // own
     for t in range(2):
         for j in range(blocks):
             for c in range(own):
                 scratch[t, j, pl.ds(c, peers, stride=own), :] = recv[
-                    pl.ds(width * j + own * t + c, peers, stride=chunk), :
+                    pl.ds(2 * own * j + own * t + c, peers, stride=chunk), :
                 ]
     conv = jnp.concatenate([scratch[0, j] for j in range(blocks)], 1)
     grad = jnp.concatenate([scratch[1, j] for j in range(blocks)], 1)
-    ext = recv[pl.ds(2 * own, chans, stride=width), :]
+    ends = recv[pl.ds(chunk - 1, peers, stride=chunk), :]
+    for c in range(own):
+        edge[pl.ds(c, peers, stride=own), :] = (
+            pltpu.roll(ends, (LANES - 4 * c) % LANES, 1) if c else ends
+        )
+    ext = edge[...]
     lane = lane_ids((chans, LANES))
     turned = pltpu.roll(ext, LANES - 2, 1)
     grad_query[0] = grad_out[0] * conv
@@ -224,10 +262,11 @@
     twice_end = jnp.where(lane < LANES - 2, twice[:, last:], turned)
     once = jnp.concatenate([once[:, :last], once_end], 1)
     twice = jnp.concatenate([twice[:, :last], twice_end], 1)
-    grad_keys[0] = tap[:, 0:1] * part + tap[:, 1:2] * once + tap[:, 2:3] * twice
-
-
-def call(body, name, outs, scratch, args, flops):
+    wide = [jnp.concatenate([t] * blocks, 1) for t in tap]
+    grad_keys[0] = wide[0] * part + wide[1] * once + wide[2] * twice
+
+
+def call(body, name, outs, scratch, args, flops, in_specs=None, room=32):
     moved = sum(a.size * a.dtype.itemsize for a in args) + sum(
         math.prod(o.shape) * o.dtype.itemsize for o in outs
     )
@@ -236,8 +275,9 @@
         out_shape=outs,
         scratch_shapes=scratch,
         name=name,
+        **({} if in_specs is None else {"in_specs": in_specs}),
         cost_estimate=pl.CostEstimate(flops=flops, bytes_accessed=moved, transcendentals=0),
-        compiler_params=pltpu.CompilerParams(vmem_limit_bytes=32 * 2**20),
+        compiler_params=pltpu.CompilerParams(vmem_limit_bytes=room * 2**20),
     )(*args)
 
 
@@ -246,9 +286,7 @@
 
 
 def exchange(x, parts):
-    rows = x.shape[0] // parts
-    assert rows % 4 == 0
-    moved = x.reshape(parts, rows // 4, 4, LANES)
+    moved = x.reshape(parts, x.shape[0] // parts, 1, LANES)
     moved = lax.all_to_all(moved, "ctx", split_axis=0, concat_axis=0, tiled=True)
     return moved.reshape(x.shape)
 
@@ -260,8 +298,11 @@
     blocks = span // LANES
     rows = length // LANES
     assert chans == own * parts and rows == LANES and blocks == own
-    packed_rows = parts * blocks * (2 * own + 1)
-    tables = make_tables(rows, LANES)
+    packed_rows = parts * (2 * own * blocks + 1)
+    order = row_order(rows, blocks)
+    places = tuple(int(n) for n in order)
+    tables = make_tables(rows, LANES, order)
+    taps = short_filter.T
     first, second, second_inv, first_inv, mid = (jnp.asarray(t) for t in tables)
     wide = 6 * LANES
     work = 6 * own * rows * wide * 2 * LANES
@@ -270,13 +311,20 @@
         functools.partial(pack_body, own, blocks),
         "pack",
         (shape(packed_rows, LANES),),
-        [tiles],
-        (grad_out, query, keys, values, short_filter),
+        [
+            pltpu.VMEM((4, chans, span), F32),
+            tiles,
+            pltpu.VMEM((chans, LANES), F32),
+            pltpu.SemaphoreType.DMA((4,)),
+        ],
+        (grad_out, query, keys, values, taps),
         10 * chans * span,
+        [pl.BlockSpec(memory_space=pltpu.HBM)] * 4 + [pl.BlockSpec(memory_space=pltpu.VMEM)],
+        60,
     )[0]
     received = exchange(packed, parts)
     spec = call(
-        filter_body,
+        functools.partial(filter_body, places),
         "filter_spectrum",
         (shape(own * rows, 2 * LANES),),
         [pltpu.VMEM((own * rows, LANES), F32), pltpu.VMEM((own * rows, wide), BF16)],
@@ -287,17 +335,13 @@
         functools.partial(main_body, own, blocks),
         "main",
         (shape(packed_rows, LANES), shape(own * rows, 2 * LANES)),
-        [
-            pltpu.VMEM((rows, LANES), F32),
-            pltpu.VMEM((own, rows, LANES), F32),
-            pltpu.VMEM((2 * own * rows, wide), BF16),
-        ],
+        [pltpu.VMEM((2 * own * rows, wide), BF16)],
         (received, spec, first, second, second_inv, first_inv, mid),
         4 * work,
     )
     returned = exchange(sent, parts)
     part = call(
-        cross_body,
+        functools.partial(cross_body, places),
         "cross",
         (shape(own, length),),
         [pltpu.VMEM((own * rows, LANES), F32), pltpu.VMEM((own * rows, wide), BF16)],
@@ -309,8 +353,8 @@
         functools.partial(finish_body, own, blocks),
         "finish",
         (shape(*keys.shape),) * 3,
-        [tiles],
-        (returned, grad_out, keys, values, short_filter),
+        [tiles, pltpu.VMEM((chans, LANES), F32)],
+        (returned, grad_out, keys, values, taps),
         10 * chans * span,
     )
     return grad_query, grad_keys, grad_values, grad_long

time: 64.6 us -> 60 us (0.929)
  local copies, waits for them, and re-layouts: 4.63 us -> 0.07 us
  Pallas kernels: 7.34 us -> 9.15 us
  waiting for transfers between devices: 30.5 us -> 28.7 us
    unnamed x27 -> x20, local copies, waits for them, and re-layouts: 4.63 us -> 0.07 us
    all_to_all x2, waiting for transfers between devices: 21 us -> 18.5 us  [exchange(): lax.all_to_all(moved, 'ctx', split_axis=0, concat_axis=0, tiled=True)]
    pallas_call x5, Pallas kernels: 7.34 us -> 9.15 us  [call(): pl.pallas_call(body, out_shape=outs, scratch_shapes=scratch, name=name, *...]
    ppermute x1, waiting for transfers between devices: 9.46 us -> 10.2 us  [shards(): grad_long = part + lax.ppermute(part, 'seq', [(0, 1), (1, 0)])]
  transfers between devices with their start and end apart: 3 -> 3, of which waited for: 3 -> 3; matrix products, arithmetic and copies ran while one was open for 1% -> 1% of each run, Pallas kernels for 2% -> 3%
where the time goes in v2:
time: 60 us; the launch traced here: 59.1 us
  waiting for transfers between devices  28.7 us (48%)
  starting transfers between devices  19.6 us (33%)
  Pallas kernels  9.15 us (15%)
  between operations  0.79 us (1%)
  other arithmetic  0.77 us (1%)
    all_to_all x2, waiting for transfers between devices, exchange(): lax.all_to_all(moved, 'ctx', split_axis=0, concat_axis=0, tiled=True)  18.5 us
    all_to_all x2, starting transfers between devices, exchange(): lax.all_to_all(moved, 'ctx', split_axis=0, concat_axis=0, tiled=True)  16.9 us
    ppermute x1, waiting for transfers between devices, shards(): grad_long = part + lax.ppermute(part, 'seq', [(0, 1), (1, 0)])  10.2 us
    pallas_call x5, Pallas kernels, call(): pl.pallas_call(body, out_shape=outs, scratch_shapes=scratch, name=name, *...  9.15 us
    ppermute x1, starting transfers between devices, shards(): grad_long = part + lax.ppermute(part, 'seq', [(0, 1), (1, 0)])  2.71 us
  transfers between devices with their start and end apart: 3, of which 3 were waited for; matrix products, arithmetic and copies ran while one was open for 1% of the time, Pallas kernels for 3%

profile of v2, /device:TPU:1, one launch (start us, length us, event | category | flops | bytes accessed | tf_op | source)
XLA Modules:
  0.0 59.1 jit_solution(13687588111205073888)
XLA Ops:
  0.6 2.9 %pack.1 = f32[1056,128]{1,0:T(8,128)} custom-call(f32[1,128,512]{2,1,0:T(8,128)} %grad_out.3, f32[1,128,512]{2,1,0:T(8,128)} %query.1, f32[1,128,512]{2,1,0:T(8,128)} %keys.3, f32[1,128,512]{2,1,0:T(8,128)} %values.3, f32[3,128]{1,0:T(4,128)} %bitcast.7), custom_call_target="tpu_custom_call" | custom-call | flops 655360 | bytes 1590784 | tf_op jit(solution)/shard_map/pack/pallas_call | solution.py:273
  3.5 0.0 copy-start.4
  3.6 0.0 copy-start.6
  3.6 0.0 copy-start.8
  3.6 0.0 copy-start.9
  3.6 11.3 %all-to-all-start = ((f32[32,33,1,128]{3,2,1,0:T(1,128)}), f32[32,33,1,128]{3,2,1,0:T(1,128)S(1)}, u32[]{:S(2)}, u32[]{:S(2)}) async-start(f32[32,33,1,128]{3,2,1,0:T(1,128)} %bitcast.9), calls=%async_computation | async-start | bytes 1081344 | tf_op jit(solution)/shard_map/all_to_all | solution.py:290
  14.9 0.0 copy-done.4
  14.9 0.0 copy-done.6
  14.9 0.0 copy-done.8
  14.9 0.0 copy-done.9
  14.9 0.0 copy-start.5
  14.9 0.0 copy-start.7
  14.9 0.8 %filter_spectrum.1.filt = f32[512,256]{1,0:T(8,128)S(1)} custom-call(f32[4,16384]{1,0:T(4,128)S(1)} %copy-done.4, bf16[256,384]{1,0:T(8,128)(2,1)S(1)} %copy-done.8, bf16[768,256]{1,0:T(8,128)(2,1)S(1)} %copy-done.6, f32[128,256]{1,0:T(8,128)S(1)} %copy-done.9), custom_call_target="tpu_custom_call" | custom-call | flops 603979776 | bytes 1507328 | tf_op jit(solution)/shard_map/filter_spectrum/pallas_call | solution.py:273
  15.7 16.0 %all-to-all-done = f32[32,33,1,128]{3,2,1,0:T(1,128)S(1)} async-done(((f32[32,33,1,128]{3,2,1,0:T(1,128)}), f32[32,33,1,128]{3,2,1,0:T(1,128)S(1)}, u32[]{:S(2)}, u32[]{:S(2)}) %all-to-all-start) | async-done | bytes 540704 | tf_op jit(solution)/shard_map/all_to_all | solution.py:290
  31.7 0.0 copy-done.5
  31.7 0.0 copy-done.7
  31.7 3.2 %main.1 = (f32[1056,128]{1,0:T(8,128)}, f32[512,256]{1,0:T(8,128)S(1)}) custom-call(f32[1056,128]{1,0:T(8,128)S(1)} %bitcast.6, f32[512,256]{1,0:T(8,128)S(1)} %filter_spectrum.1.filt, bf16[256,384]{1,0:T(8,128)(2,1)S(1)} %copy-done.8, bf16[768,256]{1,0:T(8,128)(2,1)S(1)} %copy-done.6, bf16[768,256]{1,0:T(8,128)(2,1)S(1)} %copy-done.5, ...), custom_call_target="tpu_custom_call" | custom-call | flops 2415919104 | bytes 3440640 | tf_op jit(solution)/shard_map/main/pallas_call | solution.py:273
  35.0 5.6 %all-to-all-start.1 = ((f32[32,33,1,128]{3,2,1,0:T(1,128)}), f32[32,33,1,128]{3,2,1,0:T(1,128)S(1)}, u32[]{:S(2)}, u32[]{:S(2)}) async-start(f32[32,33,1,128]{3,2,1,0:T(1,128)} %bitcast.3), calls=%async_computation.1 | async-start | bytes 1081344 | tf_op jit(solution)/shard_map/all_to_all | solution.py:290
  40.6 0.0 copy-start.3
  40.6 0.8 %cross.1 = f32[4,16384]{1,0:T(4,128)S(1)} custom-call(f32[512,256]{1,0:T(8,128)S(1)} %get-tuple-element.13.cross, bf16[768,256]{1,0:T(8,128)(2,1)S(1)} %copy-done.5, bf16[128,768]{1,0:T(8,128)(2,1)S(1)} %copy-done.7, f32[128,256]{1,0:T(8,128)S(1)} %copy-done.9), custom_call_target="tpu_custom_call" | custom-call | flops 603979776 | bytes 1507328 | tf_op jit(solution)/shard_map/cross/pallas_call | solution.py:273
  41.4 0.0 copy-start
  41.4 0.0 copy-start.1
  41.4 0.0 copy-start.2
  41.4 2.7 %collective-permute-start = (f32[4,16384]{1,0:T(4,128)S(1)}, f32[4,16384]{1,0:T(4,128)S(1)}, u32[]{:S(2)}, u32[]{:S(2)}) collective-permute-start(f32[4,16384]{1,0:T(4,128)S(1)} %cross.1), channel_id=1, source_target_pairs={{0,4},{4,0},{1,5},{5,1},{2,6},{6,2},{3,7},{7,3},{8,12},{12,8},{9,1... | collective-permute-start | bytes 786440 | tf_op jit(solution)/shard_map/ppermute | solution.py:351
  44.2 10.2 %collective-permute-done = f32[4,16384]{1,0:T(4,128)S(1)} collective-permute-done((f32[4,16384]{1,0:T(4,128)S(1)}, f32[4,16384]{1,0:T(4,128)S(1)}, u32[]{:S(2)}, u32[]{:S(2)}) %collective-permute-start) | collective-permute-done | bytes 262176 | tf_op jit(solution)/shard_map/ppermute | solution.py:351
  54.4 0.8 %add.3 = f32[4,16384]{1,0:T(4,128)} add(f32[4,16384]{1,0:T(4,128)S(1)} %cross.1, f32[4,16384]{1,0:T(4,128)S(1)} %collective-permute-done) | non-fusion elementwise | flops 65536 | bytes 786432 | tf_op jit(solution)/shard_map/add | solution.py:351
  55.2 2.4 %all-to-all-done.1 = f32[32,33,1,128]{3,2,1,0:T(1,128)S(1)} async-done(((f32[32,33,1,128]{3,2,1,0:T(1,128)}), f32[32,33,1,128]{3,2,1,0:T(1,128)S(1)}, u32[]{:S(2)}, u32[]{:S(2)}) %all-to-all-start.1) | async-done | bytes 540704 | tf_op jit(solution)/shard_map/all_to_all | solution.py:290
  57.6 0.0 copy-done.3
  57.6 0.0 copy-done
  57.6 0.0 copy-done.1
  57.6 0.0 copy-done.2
  57.6 1.4 %finish.1 = (f32[1,128,512]{2,1,0:T(8,128)}, f32[1,128,512]{2,1,0:T(8,128)}, f32[1,128,512]{2,1,0:T(8,128)}) custom-call(f32[1056,128]{1,0:T(8,128)S(1)} %bitcast.5, f32[1,128,512]{2,1,0:T(8,128)S(1)} %copy-done, f32[1,128,512]{2,1,0:T(8,128)S(1)} %copy-done.1, f32[1,128,512]{2,1,0:T(8,128)S(1)} %copy-done.2, f32[3,128]{1,0:T(4,128)S(1)} %bitcast.8), custom_call_target="tpu_custom_call" | custom-call | flops 655360 | bytes 2115072 | tf_op jit(solution)/shard_map/finish/pallas_call | solution.py:273
Async XLA Ops:
  3.5 11.3 %copy-start.4 = (f32[4,16384]{1,0:T(4,128)S(1)}, f32[4,16384]{1,0:T(4,128)}, u32[]{:S(2)}) copy-start(f32[4,16384]{1,0:T(4,128)} %long_filter.1) | copy-start | bytes 786436
  3.6 11.3 %copy-start.6 = (bf16[768,256]{1,0:T(8,128)(2,1)S(1)}, bf16[768,256]{1,0:T(8,128)(2,1)}, u32[]{:S(2)}) copy-start(bf16[768,256]{1,0:T(8,128)(2,1)} %constant.11.clone.second) | copy-start | bytes 1179652
  3.6 11.3 %copy-start.8 = (bf16[256,384]{1,0:T(8,128)(2,1)S(1)}, bf16[256,384]{1,0:T(8,128)(2,1)}, u32[]{:S(2)}) copy-start(bf16[256,384]{1,0:T(8,128)(2,1)} %constant.10.clone.first) | copy-start | bytes 589828
  3.6 11.3 %copy-start.9 = (f32[128,256]{1,0:T(8,128)S(1)}, f32[128,256]{1,0:T(8,128)}, u32[]{:S(2)}) copy-start(f32[128,256]{1,0:T(8,128)} %constant.14.clone.mid) | copy-start | bytes 393220
  3.6 28.2 %all-to-all-start = ((f32[32,33,1,128]{3,2,1,0:T(1,128)}), f32[32,33,1,128]{3,2,1,0:T(1,128)S(1)}, u32[]{:S(2)}, u32[]{:S(2)}) async-start(f32[32,33,1,128]{3,2,1,0:T(1,128)} %bitcast.9), calls=%async_computation | async-start | bytes 1081344 | tf_op jit(solution)/shard_map/all_to_all | solution.py:290
  14.9 16.8 %copy-start.5 = (bf16[768,256]{1,0:T(8,128)(2,1)S(1)}, bf16[768,256]{1,0:T(8,128)(2,1)}, u32[]{:S(2)}) copy-start(bf16[768,256]{1,0:T(8,128)(2,1)} %constant.12.clone.second_inv) | copy-start | bytes 1179652
  14.9 16.8 %copy-start.7 = (bf16[128,768]{1,0:T(8,128)(2,1)S(1)}, bf16[128,768]{1,0:T(8,128)(2,1)}, u32[]{:S(2)}) copy-start(bf16[128,768]{1,0:T(8,128)(2,1)} %constant.13.clone.first_inv) | copy-start | bytes 589828
  35.0 22.6 %all-to-all-start.1 = ((f32[32,33,1,128]{3,2,1,0:T(1,128)}), f32[32,33,1,128]{3,2,1,0:T(1,128)S(1)}, u32[]{:S(2)}, u32[]{:S(2)}) async-start(f32[32,33,1,128]{3,2,1,0:T(1,128)} %bitcast.3), calls=%async_computation.1 | async-start | bytes 1081344 | tf_op jit(solution)/shard_map/all_to_all | solution.py:290
  40.6 17.0 %copy-start.3 = (f32[128,3]{0,1:T(4,128)S(1)}, f32[128,3]{0,1:T(4,128)}, u32[]{:S(2)}) copy-start(f32[128,3]{0,1:T(4,128)} %param.16) | copy-start | bytes 4612
  41.4 16.2 %copy-start = (f32[1,128,512]{2,1,0:T(8,128)S(1)}, f32[1,128,512]{2,1,0:T(8,128)}, u32[]{:S(2)}) copy-start(f32[1,128,512]{2,1,0:T(8,128)} %grad_out.3) | copy-start | bytes 786436
  41.4 16.2 %copy-start.1 = (f32[1,128,512]{2,1,0:T(8,128)S(1)}, f32[1,128,512]{2,1,0:T(8,128)}, u32[]{:S(2)}) copy-start(f32[1,128,512]{2,1,0:T(8,128)} %keys.3) | copy-start | bytes 786436
  41.4 16.2 %copy-start.2 = (f32[1,128,512]{2,1,0:T(8,128)S(1)}, f32[1,128,512]{2,1,0:T(8,128)}, u32[]{:S(2)}) copy-start(f32[1,128,512]{2,1,0:T(8,128)} %values.3) | copy-start | bytes 786436
  41.4 12.9 %collective-permute-start = (f32[4,16384]{1,0:T(4,128)S(1)}, f32[4,16384]{1,0:T(4,128)S(1)}, u32[]{:S(2)}, u32[]{:S(2)}) collective-permute-start(f32[4,16384]{1,0:T(4,128)S(1)} %cross.1), channel_id=1, source_target_pairs={{0,4},{4,0},{1,5},{5,1},{2,6},{6,2},{3,7},{7,3},{8,12},{12,8},{9,1... | collective-permute-start | bytes 786440 | tf_op jit(solution)/shard_map/ppermute | solution.py:351

commit v3 on v2

v3 whole, which is shorter than its diff:
```python
import functools
import math

import jax
import jax.numpy as jnp
import numpy as np
from jax import lax
from jax.experimental import pallas as pl
from jax.experimental.pallas import tpu as pltpu
from jax.sharding import PartitionSpec as P

LANES = 128
F32 = jnp.float32
BF16 = jnp.bfloat16


def halves(table):
    high = table.astype(np.float32).astype(jnp.bfloat16)
    low = (table - high.astype(np.float64)).astype(np.float32).astype(jnp.bfloat16)
    return high, low


CORES = 2


def peer_order(parts):
    planes = parts // CORES // 2
    chips = [y * planes + z for z in reversed(range(planes)) for y in range(2)]
    return [CORES * chip + core for chip in chips for core in range(CORES)]


def row_order(order, blocks):
    return [blocks * s + j for j in range(blocks) for s in order]


def sorted_rows(x, order, own, back=False):
    size = CORES * own
    chips = [s // CORES for s in order[::CORES]]
    assert [CORES * chip + core for chip in chips for core in range(CORES)] == list(order)
    if back:
        chips = [chips.index(k) for k in range(len(chips))]
    return jnp.concatenate([x[size * k : size * (k + 1)] for k in chips], 0)


def make_tables(rows, cols, order):
    length = rows * cols
    shifted = np.arange(rows) + 0.25
    turn_one = 2 * np.pi * np.outer(shifted, np.array(order)) / rows
    turn_mid = 2 * np.pi * np.outer(shifted, np.arange(cols)) / length
    turn_two = 2 * np.pi * np.outer(np.arange(cols), np.arange(cols)) / cols
    cos, sin = np.cos(turn_two), np.sin(turn_two)
    first = np.concatenate([np.cos(turn_one), -np.sin(turn_one)], 0)
    second = np.block([[cos, -sin], [sin, cos]])
    second_inv = np.block([[cos, sin], [-sin, cos]])
    scale = length**-1.5
    first_inv = np.concatenate([np.cos(turn_one).T, -np.sin(turn_one).T], 1) * scale
    both = lambda m: np.concatenate(halves(m), 0)
    right = lambda m: np.concatenate([halves(m)[0], halves(m)[0], halves(m)[1]], 0)
    mid = np.concatenate([np.cos(turn_mid), -np.sin(turn_mid)], 1).astype(np.float32)
    left = lambda m: np.concatenate([halves(m)[0], halves(m)[0], halves(m)[1]], 1)
    return left(first), right(second), right(second_inv), both(first_inv), mid


def cut(x):
    high = x.astype(BF16)
    return high, (x - high.astype(F32)).astype(BF16)


def dot(a, b):
    return jnp.dot(a, b, preferred_element_type=F32)


def lane_ids(shape):
    return lax.broadcasted_iota(jnp.int32, shape, len(shape) - 1)


def row_ids(shape):
    return lax.broadcasted_iota(jnp.int32, shape, 0)


def put_cut(lhs, row, re, im):
    n = re.shape[0]
    re_hi, re_lo = cut(re)
    im_hi, im_lo = cut(im)
    for place, piece in enumerate((re_hi, im_hi, re_lo, im_lo, re_hi, im_hi)):
        lhs[pl.ds(row, n), pl.ds(place * LANES, LANES)] = piece


def left_dot(table, x):
    hi, lo = cut(x)
    rows = table.shape[0] // 2
    twice = dot(table[...], hi)
    return twice[:rows] + (twice[rows:] + dot(table[:rows], lo))


def forward(signals, first, second, mid, lhs, row):
    rows = signals[0].shape[0]
    turn_re = mid[:, :LANES]
    turn_im = mid[:, LANES:]
    for pair in range(0, len(signals), 2):
        hi, lo = cut(jnp.concatenate(signals[pair : pair + 2], 1))
        part = dot(first[...], jnp.concatenate([hi, lo, hi], 0))
        for which in range(2):
            re = part[:rows, which * LANES : (which + 1) * LANES]
            im = part[rows:, which * LANES : (which + 1) * LANES]
            put_cut(
                lhs,
                row + (pair + which) * rows,
                re * turn_re - im * turn_im,
                re * turn_im + im * turn_re,
            )
    return dot(lhs[pl.ds(row, len(signals) * rows), :], second[...])


def backward(count, rows, second_inv, first_inv, mid, lhs, row):
    turn_re = mid[:, :LANES]
    turn_im = mid[:, LANES:]
    back = dot(lhs[pl.ds(row, count * rows), :], second_inv[...])
    signals = []
    for pair in range(0, count, 2):
        columns = []
        for which in range(2):
            here = back[(pair + which) * rows : (pair + which + 1) * rows]
            re, im = here[:, :LANES], here[:, LANES:]
            columns.append(
                jnp.concatenate([re * turn_re + im * turn_im, im * turn_re - re * turn_im], 0)
            )
        out = left_dot(first_inv, jnp.concatenate(columns, 1))
        signals += [out[:, :LANES], out[:, LANES:]]
    return signals


def tap_tiles(taps):
    chans = taps.shape[1]
    return [
        jnp.transpose(jnp.broadcast_to(taps[j : j + 1, :], (LANES, chans)))
        for j in range(taps.shape[0])
    ]


def short_taps(keys, taps):
    lane = lane_ids(keys.shape)
    once = jnp.where(lane < 1, 0.0, pltpu.roll(keys, 1, 1))
    twice = jnp.where(lane < 2, 0.0, pltpu.roll(keys, 2, 1))
    wide = [jnp.concatenate([t] * (keys.shape[1] // LANES), 1) for t in taps]
    return wide[0] * keys + wide[1] * once + wide[2] * twice


def pack_body(
    own, blocks, order, grad_out, query, keys, values, taps, out, held, few, scratch, edge, rows, sems
):
    copies = [pltpu.make_async_copy(taps, few, sems.at[4])] + [
        pltpu.make_async_copy(source.at[0], held.at[i], sems.at[i])
        for i, source in enumerate((keys, values, grad_out, query))
    ]
    for copy in copies:
        copy.start()
    chunk = 2 * own * blocks + 1
    chans, span = keys.shape[1:]
    peers = chans // own
    copies[0].wait()
    tap = tap_tiles(few)
    copies[1].wait()
    copies[2].wait()
    key, value = held[0], held[1]
    gated = short_taps(key, tap) * value
    lane = lane_ids((chans, LANES))
    tail = key[:, span - LANES :]
    after = tap[2] * pltpu.roll(tail, 2, 1) + jnp.where(
        lane < 1, tap[1] * pltpu.roll(tail, 1, 1), 0.0
    )
    head = jnp.where(lane < 4, pltpu.roll(value[:, :LANES], 2, 1), 0.0)
    edge[...] = sorted_rows(jnp.where(lane < 2, after, head), order, own)
    for j in range(blocks):
        scratch[0, j] = sorted_rows(gated[:, j * LANES : (j + 1) * LANES], order, own)
    copies[3].wait()
    copies[4].wait()
    for j in range(blocks):
        here = slice(j * LANES, (j + 1) * LANES)
        scratch[1, j] = sorted_rows(held[2, :, here] * held[3, :, here], order, own)
    half = peers // 2
    writes = []
    for part in range(2):
        start = part * half * chunk
        lines = lambda c: pl.ds(part * half * own + c, half, stride=own)
        for t in range(2):
            for j in range(blocks):
                for c in range(own):
                    place = start + 2 * own * j + own * t + c
                    rows[pl.ds(place, half, stride=chunk), :] = scratch[t, j, lines(c), :]
        ends = edge[lines(0), :]
        for c in range(1, own):
            ends = ends + pltpu.roll(edge[lines(c), :], 4 * c, 1)
        rows[pl.ds(start + chunk - 1, half, stride=chunk), :] = ends
        piece = pl.ds(start, half * chunk)
        writes.append(pltpu.make_async_copy(rows.at[piece], out.at[piece], sems.at[5 + part]))
        writes[-1].start()
    for write in writes:
        write.wait()


def filter_body(order, long_filter, first, second, mid, spec, scratch, lhs):
    own, length = long_filter.shape
    rows = length // LANES
    for n, place in enumerate(order):
        scratch[pl.ds(own * n, own), :] = long_filter[:, pl.ds(place * LANES, LANES)]
    signals = [scratch[pl.ds(c, rows, stride=own), :] for c in range(own)]
    spec[...] = forward(signals, first, second, mid, lhs, 0)


def main_body(
    own, blocks, order, recv, filt, first, second, second_inv, first_inv, mid, out, cross, past, next_, lhs, back
):
    chunk = 2 * own * blocks + 1
    peers = recv.shape[0] // chunk
    rows = peers * blocks
    place = lambda t, j, c: pl.ds(2 * own * j + own * t + c, peers, stride=chunk)
    ends = recv[pl.ds(chunk - 1, peers, stride=chunk), :]
    lane = lane_ids(ends.shape)
    for i, s in enumerate(order):
        row = jnp.zeros((1, LANES), F32)
        if s:
            row = recv[pl.ds(chunk * order.index(s - 1) + chunk - 1, 1), :]
        past[pl.ds(i, 1), :] = row
    before = past[...]
    heads, gates, grads = [], [], []
    for c in range(own):
        heads.append(
            jnp.where(lane < 2, pltpu.roll(ends, (LANES - 4 * c - 2) % LANES, 1), 0.0)
        )
        mine = pltpu.roll(before, (LANES - 4 * c) % LANES, 1) if c else before
        tiles = [recv[place(0, j, c), :] for j in range(blocks)]
        tiles[0] = tiles[0] + heads[c] * mine
        gates.append(jnp.concatenate(tiles, 0))
        grads.append(jnp.concatenate([recv[place(1, j, c), :] for j in range(blocks)], 0))
    spec = forward(gates + grads, first, second, mid, lhs, 0)
    gate, grad = spec[: own * rows], spec[own * rows :]
    for c in range(own):
        here = slice(c * rows, (c + 1) * rows)
        g_re, g_im = gate[here, :LANES], gate[here, LANES:]
        d_re, d_im = grad[here, :LANES], grad[here, LANES:]
        f_re, f_im = filt[here, :LANES], filt[here, LANES:]
        put_cut(back, c * rows, g_re * f_re - g_im * f_im, g_re * f_im + g_im * f_re)
        put_cut(back, (own + c) * rows, d_re * f_re + d_im * f_im, d_im * f_re - d_re * f_im)
        cross[here, :LANES] = d_re * g_re + d_im * g_im
        cross[here, LANES:] = d_im * g_re - d_re * g_im
    signals = backward(2 * own, rows, second_inv, first_inv, mid, back, 0)
    for q, signal in enumerate(signals):
        for j in range(blocks):
            out[place(q // own, j, q % own), :] = signal[j * peers : (j + 1) * peers]
    behind = signals[own][:peers] * heads[0]
    for c in range(1, own):
        behind = behind + pltpu.roll(signals[own + c][:peers] * heads[c], 4 * c, 1)
    past[...] = behind
    for i, s in enumerate(order):
        row = jnp.zeros((1, LANES), F32)
        if s + 1 < peers:
            row = past[pl.ds(order.index(s + 1), 1), :]
        next_[pl.ds(i, 1), :] = row
    out[pl.ds(chunk - 1, peers, stride=chunk), :] = jnp.where(
        lane % 4 < 2, next_[...], pltpu.roll(before, 2, 1)
    )


def cross_body(order, cross, second_inv, first_inv, mid, part, scratch, lhs):
    own, length = part.shape
    rows = length // LANES
    for c in range(own):
        here = slice(c * rows, (c + 1) * rows)
        put_cut(lhs, c * rows, cross[here, :LANES], cross[here, LANES:])
    for c, signal in enumerate(backward(own, rows, second_inv, first_inv, mid, lhs, 0)):
        scratch[pl.ds(c, rows, stride=own), :] = signal
    for n, place in enumerate(order):
        part[:, pl.ds(place * LANES, LANES)] = scratch[pl.ds(own * n, own), :]


def finish_body(
    own, blocks, order, recv, grad_out, keys, values, taps, grad_query, grad_keys, grad_values, scratch, edge, held, sems
):
    chunk = 2 * own * blocks + 1
    tap = tap_tiles(taps)
    chans, span = keys.shape[1:]
    peers = chans // own
    lane = lane_ids((chans, LANES))
    tile = lambda x, j: x[0, :, j * LANES : (j + 1) * LANES]

    def gathered(t, j):
        for c in range(own):
            scratch[t, j, pl.ds(c, peers, stride=own), :] = recv[
                pl.ds(2 * own * j + own * t + c, peers, stride=chunk), :
            ]
        return sorted_rows(scratch[t, j], order, own, back=True)

    writes = [
        pltpu.make_async_copy(held.at[i], out.at[0], sems.at[i])
        for i, out in enumerate((grad_query, grad_values, grad_keys))
    ]
    for j in range(blocks):
        held[0, :, j * LANES : (j + 1) * LANES] = tile(grad_out, j) * gathered(0, j)
    writes[0].start()
    ends = recv[pl.ds(chunk - 1, peers, stride=chunk), :]
    for c in range(own):
        edge[pl.ds(c, peers, stride=own), :] = (
            pltpu.roll(ends, (LANES - 4 * c) % LANES, 1) if c else ends
        )
    ext = sorted_rows(edge[...], order, own, back=True)
    turned = pltpu.roll(ext, LANES - 2, 1)
    parts = []
    back_one = back_two = None
    for j in range(blocks):
        key = tile(keys, j)
        one, two = pltpu.roll(key, 1, 1), pltpu.roll(key, 2, 1)
        if j:
            once = jnp.where(lane < 1, back_one, one)
            twice = jnp.where(lane < 2, back_two, two)
        else:
            once = jnp.where(lane < 1, 0.0, one)
            twice = jnp.where(lane < 2, 0.0, two)
        back_one, back_two = one, two
        short = tap[0] * key + tap[1] * once + tap[2] * twice
        if not j:
            short = short + jnp.where(lane < 2, turned, 0.0)
        grad = gathered(1, j)
        held[1, :, j * LANES : (j + 1) * LANES] = grad * short
        parts.append(grad * tile(values, j))
    writes[1].start()
    ahead_one, ahead_two = pltpu.roll(ext, LANES - 1, 1), turned
    for j in reversed(range(blocks)):
        one, two = pltpu.roll(parts[j], LANES - 1, 1), pltpu.roll(parts[j], LANES - 2, 1)
        once = jnp.where(lane < LANES - 1, one, ahead_one)
        twice = jnp.where(lane < LANES - 2, two, ahead_two)
        ahead_one, ahead_two = one, two
        held[2, :, j * LANES : (j + 1) * LANES] = (
            tap[0] * parts[j] + tap[1] * once + tap[2] * twice
        )
    writes[2].start()
    for write in writes:
        write.wait()


def call(body, name, outs, scratch, args, flops, room=32, **specs):
    moved = sum(a.size * a.dtype.itemsize for a in args) + sum(
        math.prod(o.shape) * o.dtype.itemsize for o in outs
    )
    return pl.pallas_call(
        body,
        out_shape=outs,
        scratch_shapes=scratch,
        name=name,
        **specs,
        cost_estimate=pl.CostEstimate(flops=flops, bytes_accessed=moved, transcendentals=0),
        compiler_params=pltpu.CompilerParams(vmem_limit_bytes=room * 2**20),
    )(*args)


def shape(*dims):
    return jax.ShapeDtypeStruct(dims, F32)


def exchange(x, order):
    parts = len(order)
    moved = x.reshape(parts, x.shape[0] // parts, 1, LANES)
    moved = lax.all_to_all(moved, "ctx", split_axis=0, concat_axis=0, axis_index_groups=[order], tiled=True)
    return moved.reshape(x.shape)


def shards(grad_out, query, keys, values, long_filter, short_filter):
    _, chans, span = keys.shape
    own, length = long_filter.shape
    parts = length // span
    blocks = span // LANES
    rows = length // LANES
    assert chans == own * parts and rows == LANES and blocks == own
    packed_rows = parts * (2 * own * blocks + 1)
    order = peer_order(parts)
    places = row_order(order, blocks)
    tables = make_tables(rows, LANES, places)
    taps = short_filter.T
    first, second, second_inv, first_inv, mid = (jnp.asarray(t) for t in tables)
    wide = 6 * LANES
    work = 6 * own * rows * wide * 2 * LANES
    in_hbm = pl.BlockSpec(memory_space=pltpu.HBM)
    tiles = pltpu.VMEM((2, blocks, chans, LANES), F32)
    packed = call(
        functools.partial(pack_body, own, blocks, order),
        "pack",
        (shape(packed_rows, LANES),),
        [
            pltpu.VMEM((4, chans, span), F32),
            pltpu.VMEM(taps.shape, F32),
            tiles,
            pltpu.VMEM((chans, LANES), F32),
            pltpu.VMEM((packed_rows, LANES), F32),
            pltpu.SemaphoreType.DMA((7,)),
        ],
        (grad_out, query, keys, values, taps),
        10 * chans * span,
        60,
        in_specs=[in_hbm] * 5,
        out_specs=(in_hbm,),
    )[0]
    received = exchange(packed, order)
    spec = call(
        functools.partial(filter_body, places),
        "filter_spectrum",
        (shape(own * rows, 2 * LANES),),
        [pltpu.VMEM((own * rows, LANES), F32), pltpu.VMEM((own * rows, wide), BF16)],
        (long_filter, first, second, mid),
        work,
    )[0]
    sent, cross = call(
        functools.partial(main_body, own, blocks, order),
        "main",
        (shape(packed_rows, LANES), shape(own * rows, 2 * LANES)),
        [pltpu.VMEM((parts, LANES), F32)] * 2 + [pltpu.VMEM((2 * own * rows, wide), BF16)] * 2,
        (received, spec, first, second, second_inv, first_inv, mid),
        4 * work,
    )
    returned = exchange(sent, order)
    part = call(
        functools.partial(cross_body, places),
        "cross",
        (shape(own, length),),
        [pltpu.VMEM((own * rows, LANES), F32), pltpu.VMEM((own * rows, wide), BF16)],
        (cross, second_inv, first_inv, mid),
        work,
    )[0]
    grad_long = part + lax.ppermute(part, "seq", [(0, 1), (1, 0)])
    grad_query, grad_keys, grad_values = call(
        functools.partial(finish_body, own, blocks, order),
        "finish",
        (shape(*keys.shape),) * 3,
        [
            tiles,
            pltpu.VMEM((chans, LANES), F32),
            pltpu.VMEM((3, chans, span), F32),
            pltpu.SemaphoreType.DMA((3,)),
        ],
        (returned, grad_out, keys, values, taps),
        10 * chans * span,
        out_specs=(in_hbm,) * 3,
    )
    return grad_query, grad_keys, grad_values, grad_long


def solution(mesh):
    block = P("seq", "ch", "ctx")
    rows = P(("ch", "ctx"), None)
    return jax.shard_map(
        shards,
        mesh=mesh,
        in_specs=(block, block, block, block, rows, P("ch", None)),
        out_specs=(block, block, block, rows),
        check_vma=False,
    )
```

time: 60 us -> 56.6 us (0.943); the launches traced: 59.1 us -> 56.3 us
  waiting for transfers between devices: 28.7 us -> 24.2 us
  starting transfers between devices: 19.6 us -> 22.1 us
  Pallas kernels: 9.15 us -> 8.43 us
    all_to_all x2, waiting for transfers between devices: 18.5 us -> 13.2 us  [exchange(): lax.all_to_all(moved, 'ctx', split_axis=0, concat_axis=0, axis_index_grou...]
    all_to_all x2, starting transfers between devices: 16.9 us -> 19.4 us  [exchange(): lax.all_to_all(moved, 'ctx', split_axis=0, concat_axis=0, axis_index_grou...]
    ppermute x1, waiting for transfers between devices: 10.2 us -> 11 us  [shards(): grad_long = part + lax.ppermute(part, 'seq', [(0, 1), (1, 0)])]
    pallas_call x5, Pallas kernels: 9.15 us -> 8.43 us  [call(): pl.pallas_call(body, out_shape=outs, scratch_shapes=scratch, name=name, *...]
  transfers between devices with their start and end apart: 3 -> 3, of which waited for: 3 -> 2; matrix products, arithmetic and copies ran while one was open for 1% -> 1% of each run, Pallas kernels for 3% -> 3%
where the time goes in v3:
time: 56.6 us; the launch traced here: 56.3 us
  waiting for transfers between devices  24.2 us (43%)
  starting transfers between devices  22.1 us (39%)
  Pallas kernels  8.43 us (15%)
  between operations  0.8 us (1%)
  other arithmetic  0.77 us (1%)
    all_to_all x2, starting transfers between devices, exchange(): lax.all_to_all(moved, 'ctx', split_axis=0, concat_axis=0, axis_index_grou...  19.4 us
    all_to_all x2, waiting for transfers between devices, exchange(): lax.all_to_all(moved, 'ctx', split_axis=0, concat_axis=0, axis_index_grou...  13.2 us
    ppermute x1, waiting for transfers between devices, shards(): grad_long = part + lax.ppermute(part, 'seq', [(0, 1), (1, 0)])  11 us
    pallas_call x5, Pallas kernels, call(): pl.pallas_call(body, out_shape=outs, scratch_shapes=scratch, name=name, *...  8.43 us
    ppermute x1, starting transfers between devices, shards(): grad_long = part + lax.ppermute(part, 'seq', [(0, 1), (1, 0)])  2.71 us
  transfers between devices with their start and end apart: 3, of which 2 were waited for; matrix products, arithmetic and copies ran while one was open for 1% of the time, Pallas kernels for 3%

profile of v3, /device:TPU:1, one launch (start us, length us, event | category | flops | bytes accessed | tf_op | source)
XLA Modules:
  0.0 56.3 jit_solution(595389151315588440)
XLA Ops:
  0.6 2.2 %pack.1 = f32[1056,128]{1,0:T(8,128)} custom-call(f32[1,128,512]{2,1,0:T(8,128)} %grad_out.3, f32[1,128,512]{2,1,0:T(8,128)} %query.1, f32[1,128,512]{2,1,0:T(8,128)} %keys.3, f32[1,128,512]{2,1,0:T(8,128)} %values.3, f32[3,128]{1,0:T(4,128)} %bitcast.7), custom_call_target="tpu_custom_call" | custom-call | flops 655360 | bytes 1590784 | tf_op jit(solution)/shard_map/pack/pallas_call | solution.py:345
  2.9 0.0 copy-start.4
  2.9 0.0 copy-start.6
  2.9 0.0 copy-start.7
  2.9 0.0 copy-start.8
  2.9 11.5 %all-to-all-start = ((f32[32,33,1,128]{3,2,1,0:T(1,128)}), f32[32,33,1,128]{3,2,1,0:T(1,128)S(1)}, u32[]{:S(2)}, u32[]{:S(2)}) async-start(f32[32,33,1,128]{3,2,1,0:T(1,128)} %bitcast.9), calls=%async_computation | async-start | bytes 1081344 | tf_op jit(solution)/shard_map/all_to_all | solution.py:363
  14.4 0.0 copy-done.4
  14.4 0.0 copy-done.6
  14.5 0.0 copy-done.7
  14.5 0.0 copy-done.8
  14.5 0.0 copy-start.5
  14.5 0.0 copy-start.9
  14.5 0.8 %filter_spectrum.1.filt = f32[512,256]{1,0:T(8,128)S(1)} custom-call(f32[4,16384]{1,0:T(4,128)S(1)} %copy-done.4, bf16[256,384]{1,0:T(8,128)(2,1)S(1)} %copy-done.7, bf16[768,256]{1,0:T(8,128)(2,1)S(1)} %copy-done.6, f32[128,256]{1,0:T(8,128)S(1)} %copy-done.8), custom_call_target="tpu_custom_call" | custom-call | flops 603979776 | bytes 1507328 | tf_op jit(solution)/shard_map/filter_spectrum/pallas_call | solution.py:345
  15.3 13.2 %all-to-all-done = f32[32,33,1,128]{3,2,1,0:T(1,128)S(1)} async-done(((f32[32,33,1,128]{3,2,1,0:T(1,128)}), f32[32,33,1,128]{3,2,1,0:T(1,128)S(1)}, u32[]{:S(2)}, u32[]{:S(2)}) %all-to-all-start) | async-done | bytes 540704 | tf_op jit(solution)/shard_map/all_to_all | solution.py:363
  28.5 0.0 copy-done.5
  28.5 0.0 copy-done.9
  28.5 3.3 %main.1 = (f32[1056,128]{1,0:T(8,128)}, f32[512,256]{1,0:T(8,128)S(1)}) custom-call(f32[1056,128]{1,0:T(8,128)S(1)} %bitcast.6, f32[512,256]{1,0:T(8,128)S(1)} %filter_spectrum.1.filt, bf16[256,384]{1,0:T(8,128)(2,1)S(1)} %copy-done.7, bf16[768,256]{1,0:T(8,128)(2,1)S(1)} %copy-done.6, bf16[768,256]{1,0:T(8,128)(2,1)S(1)} %copy-done.5, ...), custom_call_target="tpu_custom_call" | custom-call | flops 2415919104 | bytes 3375104 | tf_op jit(solution)/shard_map/main/pallas_call | solution.py:345
  31.8 7.9 %all-to-all-start.1 = ((f32[32,33,1,128]{3,2,1,0:T(1,128)}), f32[32,33,1,128]{3,2,1,0:T(1,128)S(1)}, u32[]{:S(2)}, u32[]{:S(2)}) async-start(f32[32,33,1,128]{3,2,1,0:T(1,128)} %bitcast.3), calls=%async_computation.1 | async-start | bytes 1081344 | tf_op jit(solution)/shard_map/all_to_all | solution.py:363
  39.7 0.0 copy-start.3
  39.7 0.8 %cross.1 = f32[4,16384]{1,0:T(4,128)S(1)} custom-call(f32[512,256]{1,0:T(8,128)S(1)} %get-tuple-element.13.cross, bf16[768,256]{1,0:T(8,128)(2,1)S(1)} %copy-done.5, bf16[256,256]{1,0:T(8,128)(2,1)S(1)} %copy-done.9, f32[128,256]{1,0:T(8,128)S(1)} %copy-done.8), custom_call_target="tpu_custom_call" | custom-call | flops 603979776 | bytes 1441792 | tf_op jit(solution)/shard_map/cross/pallas_call | solution.py:345
  40.5 0.0 copy-start
  40.5 0.0 copy-start.1
  40.5 0.0 copy-start.2
  40.5 2.7 %collective-permute-start = (f32[4,16384]{1,0:T(4,128)S(1)}, f32[4,16384]{1,0:T(4,128)S(1)}, u32[]{:S(2)}, u32[]{:S(2)}) collective-permute-start(f32[4,16384]{1,0:T(4,128)S(1)} %cross.1), channel_id=1, source_target_pairs={{0,4},{4,0},{1,5},{5,1},{2,6},{6,2},{3,7},{7,3},{8,12},{12,8},{9,1... | collective-permute-start | bytes 786440 | tf_op jit(solution)/shard_map/ppermute | solution.py:428
  43.2 11.0 %collective-permute-done = f32[4,16384]{1,0:T(4,128)S(1)} collective-permute-done((f32[4,16384]{1,0:T(4,128)S(1)}, f32[4,16384]{1,0:T(4,128)S(1)}, u32[]{:S(2)}, u32[]{:S(2)}) %collective-permute-start) | collective-permute-done | bytes 262176 | tf_op jit(solution)/shard_map/ppermute | solution.py:428
  54.2 0.8 %add.3 = f32[4,16384]{1,0:T(4,128)} add(f32[4,16384]{1,0:T(4,128)S(1)} %cross.1, f32[4,16384]{1,0:T(4,128)S(1)} %collective-permute-done) | non-fusion elementwise | flops 65536 | bytes 786432 | tf_op jit(solution)/shard_map/add | solution.py:428
  55.0 0.0 all-to-all-done.1
  55.0 0.0 copy-done.3
  55.0 0.0 copy-done
  55.0 0.0 copy-done.1
  55.0 0.0 copy-done.2
  55.0 1.3 %finish.1 = (f32[1,128,512]{2,1,0:T(8,128)}, f32[1,128,512]{2,1,0:T(8,128)}, f32[1,128,512]{2,1,0:T(8,128)}) custom-call(f32[1056,128]{1,0:T(8,128)S(1)} %bitcast.5, f32[1,128,512]{2,1,0:T(8,128)S(1)} %copy-done, f32[1,128,512]{2,1,0:T(8,128)S(1)} %copy-done.1, f32[1,128,512]{2,1,0:T(8,128)S(1)} %copy-done.2, f32[3,128]{1,0:T(4,128)S(1)} %bitcast.8), custom_call_target="tpu_custom_call" | custom-call | flops 655360 | bytes 2115072 | tf_op jit(solution)/shard_map/finish/pallas_call | solution.py:345
Async XLA Ops:
  2.9 11.6 %copy-start.4 = (f32[4,16384]{1,0:T(4,128)S(1)}, f32[4,16384]{1,0:T(4,128)}, u32[]{:S(2)}) copy-start(f32[4,16384]{1,0:T(4,128)} %long_filter.1) | copy-start | bytes 786436
  2.9 11.6 %copy-start.6 = (bf16[768,256]{1,0:T(8,128)(2,1)S(1)}, bf16[768,256]{1,0:T(8,128)(2,1)}, u32[]{:S(2)}) copy-start(bf16[768,256]{1,0:T(8,128)(2,1)} %constant.11.clone.second) | copy-start | bytes 1179652
  2.9 11.6 %copy-start.7 = (bf16[256,384]{1,0:T(8,128)(2,1)S(1)}, bf16[256,384]{1,0:T(8,128)(2,1)}, u32[]{:S(2)}) copy-start(bf16[256,384]{1,0:T(8,128)(2,1)} %constant.10.clone.first) | copy-start | bytes 589828
  2.9 11.6 %copy-start.8 = (f32[128,256]{1,0:T(8,128)S(1)}, f32[128,256]{1,0:T(8,128)}, u32[]{:S(2)}) copy-start(f32[128,256]{1,0:T(8,128)} %constant.14.clone.mid) | copy-start | bytes 393220
  2.9 25.6 %all-to-all-start = ((f32[32,33,1,128]{3,2,1,0:T(1,128)}), f32[32,33,1,128]{3,2,1,0:T(1,128)S(1)}, u32[]{:S(2)}, u32[]{:S(2)}) async-start(f32[32,33,1,128]{3,2,1,0:T(1,128)} %bitcast.9), calls=%async_computation | async-start | bytes 1081344 | tf_op jit(solution)/shard_map/all_to_all | solution.py:363
  14.5 14.0 %copy-start.5 = (bf16[768,256]{1,0:T(8,128)(2,1)S(1)}, bf16[768,256]{1,0:T(8,128)(2,1)}, u32[]{:S(2)}) copy-start(bf16[768,256]{1,0:T(8,128)(2,1)} %constant.12.clone.second_inv) | copy-start | bytes 1179652
  14.5 14.0 %copy-start.9 = (bf16[256,256]{1,0:T(8,128)(2,1)S(1)}, bf16[256,256]{1,0:T(8,128)(2,1)}, u32[]{:S(2)}) copy-start(bf16[256,256]{1,0:T(8,128)(2,1)} %constant.13.clone.first_inv) | copy-start | bytes 393220
  31.8 23.2 %all-to-all-start.1 = ((f32[32,33,1,128]{3,2,1,0:T(1,128)}), f32[32,33,1,128]{3,2,1,0:T(1,128)S(1)}, u32[]{:S(2)}, u32[]{:S(2)}) async-start(f32[32,33,1,128]{3,2,1,0:T(1,128)} %bitcast.3), calls=%async_computation.1 | async-start | bytes 1081344 | tf_op jit(solution)/shard_map/all_to_all | solution.py:363
  39.7 15.3 %copy-start.3 = (f32[128,3]{0,1:T(4,128)S(1)}, f32[128,3]{0,1:T(4,128)}, u32[]{:S(2)}) copy-start(f32[128,3]{0,1:T(4,128)} %param.16) | copy-start | bytes 4612
  40.5 14.5 %copy-start = (f32[1,128,512]{2,1,0:T(8,128)S(1)}, f32[1,128,512]{2,1,0:T(8,128)}, u32[]{:S(2)}) copy-start(f32[1,128,512]{2,1,0:T(8,128)} %grad_out.3) | copy-start | bytes 786436
  40.5 14.5 %copy-start.1 = (f32[1,128,512]{2,1,0:T(8,128)S(1)}, f32[1,128,512]{2,1,0:T(8,128)}, u32[]{:S(2)}) copy-start(f32[1,128,512]{2,1,0:T(8,128)} %keys.3) | copy-start | bytes 786436
  40.5 14.5 %copy-start.2 = (f32[1,128,512]{2,1,0:T(8,128)S(1)}, f32[1,128,512]{2,1,0:T(8,128)}, u32[]{:S(2)}) copy-start(f32[1,128,512]{2,1,0:T(8,128)} %values.3) | copy-start | bytes 786436
  40.5 13.7 %collective-permute-start = (f32[4,16384]{1,0:T(4,128)S(1)}, f32[4,16384]{1,0:T(4,128)S(1)}, u32[]{:S(2)}, u32[]{:S(2)}) collective-permute-start(f32[4,16384]{1,0:T(4,128)S(1)} %cross.1), channel_id=1, source_target_pairs={{0,4},{4,0},{1,5},{5,1},{2,6},{6,2},{3,7},{7,3},{8,12},{12,8},{9,1... | collective-permute-start | bytes 786440 | tf_op jit(solution)/shard_map/ppermute | solution.py:428

commit v4 on v3

--- a/solution.py
+++ b/solution.py
@@ -55,10 +55,9 @@
     scale = length**-1.5
     first_inv = np.concatenate([np.cos(turn_one).T, -np.sin(turn_one).T], 1) * scale
     both = lambda m: np.concatenate(halves(m), 0)
-    right = lambda m: np.concatenate([halves(m)[0], halves(m)[0], halves(m)[1]], 0)
     mid = np.concatenate([np.cos(turn_mid), -np.sin(turn_mid)], 1).astype(np.float32)
     left = lambda m: np.concatenate([halves(m)[0], halves(m)[0], halves(m)[1]], 1)
-    return left(first), right(second), right(second_inv), both(first_inv), mid
+    return left(first), both(second), both(second_inv), both(first_inv), mid
 
 
 def cut(x):
@@ -82,7 +81,7 @@
     n = re.shape[0]
     re_hi, re_lo = cut(re)
     im_hi, im_lo = cut(im)
-    for place, piece in enumerate((re_hi, im_hi, re_lo, im_lo, re_hi, im_hi)):
+    for place, piece in enumerate((re_hi, im_hi, re_lo, im_lo)):
         lhs[pl.ds(row, n), pl.ds(place * LANES, LANES)] = piece
 
 
@@ -91,6 +90,19 @@
     rows = table.shape[0] // 2
     twice = dot(table[...], hi)
     return twice[:rows] + (twice[rows:] + dot(table[:rows], lo))
+
+
+def rows_dot(lhs, row, count, table):
+    half = count // 2
+    wide = 2 * LANES
+    parts = []
+    for k in range(2):
+        x = lhs[pl.ds(row + k * half, half), :]
+        high, low = x[:, :wide], x[:, wide:]
+        parts.append(
+            dot(high, table[:wide]) + dot(low, table[:wide]) + dot(high, table[wide:])
+        )
+    return jnp.concatenate(parts, 0)
 
 
 def forward(signals, first, second, mid, lhs, row):
@@ -99,7 +111,9 @@
     turn_im = mid[:, LANES:]
     for pair in range(0, len(signals), 2):
         hi, lo = cut(jnp.concatenate(signals[pair : pair + 2], 1))
-        part = dot(first[...], jnp.concatenate([hi, lo, hi], 0))
+        part = dot(first[:, : 2 * rows], jnp.concatenate([hi, lo], 0)) + dot(
+            first[:, 2 * rows :], hi
+        )
         for which in range(2):
             re = part[:rows, which * LANES : (which + 1) * LANES]
             im = part[rows:, which * LANES : (which + 1) * LANES]
@@ -109,13 +123,13 @@
                 re * turn_re - im * turn_im,
                 re * turn_im + im * turn_re,
             )
-    return dot(lhs[pl.ds(row, len(signals) * rows), :], second[...])
+    return rows_dot(lhs, row, len(signals) * rows, second)
 
 
 def backward(count, rows, second_inv, first_inv, mid, lhs, row):
     turn_re = mid[:, :LANES]
     turn_im = mid[:, LANES:]
-    back = dot(lhs[pl.ds(row, count * rows), :], second_inv[...])
+    back = rows_dot(lhs, row, count * rows, second_inv)
     signals = []
     for pair in range(0, count, 2):
         columns = []
@@ -275,7 +289,7 @@
 
 
 def finish_body(
-    own, blocks, order, recv, grad_out, keys, values, taps, grad_query, grad_keys, grad_values, scratch, edge, held, sems
+    own, blocks, order, recv, grad_out, keys, values, taps, part, other, grad_query, grad_keys, grad_values, grad_long, scratch, edge, held, total, sems
 ):
     chunk = 2 * own * blocks + 1
     tap = tap_tiles(taps)
@@ -294,7 +308,9 @@
     writes = [
         pltpu.make_async_copy(held.at[i], out.at[0], sems.at[i])
         for i, out in enumerate((grad_query, grad_values, grad_keys))
-    ]
+    ] + [pltpu.make_async_copy(total, grad_long, sems.at[3])]
+    total[...] = part[...] + other[...]
+    writes[3].start()
     for j in range(blocks):
         held[0, :, j * LANES : (j + 1) * LANES] = tile(grad_out, j) * gathered(0, j)
     writes[0].start()
@@ -377,8 +393,8 @@
     tables = make_tables(rows, LANES, places)
     taps = short_filter.T
     first, second, second_inv, first_inv, mid = (jnp.asarray(t) for t in tables)
-    wide = 6 * LANES
-    work = 6 * own * rows * wide * 2 * LANES
+    wide = 4 * LANES
+    work = 36 * own * rows * LANES * 2 * LANES
     in_hbm = pl.BlockSpec(memory_space=pltpu.HBM)
     tiles = pltpu.VMEM((2, blocks, chans, LANES), F32)
     packed = call(
@@ -425,20 +441,21 @@
         (cross, second_inv, first_inv, mid),
         work,
     )[0]
-    grad_long = part + lax.ppermute(part, "seq", [(0, 1), (1, 0)])
-    grad_query, grad_keys, grad_values = call(
+    other = lax.ppermute(part, "seq", [(0, 1), (1, 0)])
+    grad_query, grad_keys, grad_values, grad_long = call(
         functools.partial(finish_body, own, blocks, order),
         "finish",
-        (shape(*keys.shape),) * 3,
+        (shape(*keys.shape),) * 3 + (shape(own, length),),
         [
             tiles,
             pltpu.VMEM((chans, LANES), F32),
             pltpu.VMEM((3, chans, span), F32),
-            pltpu.SemaphoreType.DMA((3,)),
+            pltpu.VMEM((own, length), F32),
+            pltpu.SemaphoreType.DMA((4,)),
         ],
-        (returned, grad_out, keys, values, taps),
+        (returned, grad_out, keys, values, taps, part, other),
         10 * chans * span,
-        out_specs=(in_hbm,) * 3,
+        out_specs=(in_hbm,) * 4,
     )
     return grad_query, grad_keys, grad_values, grad_long
 

time: 56.6 us -> 55.3 us (0.977)
  other arithmetic: 0.77 us -> 0 us
  Pallas kernels: 8.43 us -> 7.72 us
    add x1 -> x0, other arithmetic: 0.77 us -> none  [shards(): grad_long = part + lax.ppermute(part, 'seq', [(0, 1), (1, 0)])]
    pallas_call x5, Pallas kernels: 8.43 us -> 7.72 us  [call(): pl.pallas_call(body, out_shape=outs, scratch_shapes=scratch, name=name, *...]
  transfers between devices with their start and end apart: 3 -> 3, of which waited for: 2 -> 2; matrix products, arithmetic and copies ran while one was open for 1% -> 0% of each run, Pallas kernels for 3% -> 3%
where the time goes in v4:
time: 55.3 us; the launch traced here: 55 us
  waiting for transfers between devices  24.3 us (44%)
  starting transfers between devices  22.1 us (40%)
  Pallas kernels  7.72 us (14%)
  between operations  0.8 us (1%)
    all_to_all x2, starting transfers between devices, exchange(): lax.all_to_all(moved, 'ctx', split_axis=0, concat_axis=0, axis_index_grou...  19.4 us
    all_to_all x2, waiting for transfers between devices, exchange(): lax.all_to_all(moved, 'ctx', split_axis=0, concat_axis=0, axis_index_grou...  13.2 us
    ppermute x1, waiting for transfers between devices, shards(): other = lax.ppermute(part, 'seq', [(0, 1), (1, 0)])  11.1 us
    pallas_call x5, Pallas kernels, call(): pl.pallas_call(body, out_shape=outs, scratch_shapes=scratch, name=name, *...  7.72 us
    ppermute x1, starting transfers between devices, shards(): other = lax.ppermute(part, 'seq', [(0, 1), (1, 0)])  2.71 us
  transfers between devices with their start and end apart: 3, of which 2 were waited for; matrix products, arithmetic and copies ran while one was open for 0% of the time, Pallas kernels for 3%

profile of v4, /device:TPU:1, one launch (start us, length us, event | category | flops | bytes accessed | tf_op | source)
XLA Modules:
  0.0 55.0 jit_solution(8388882488745016296)
XLA Ops:
  0.6 2.2 %pack.1 = f32[1056,128]{1,0:T(8,128)} custom-call(f32[1,128,512]{2,1,0:T(8,128)} %grad_out.3, f32[1,128,512]{2,1,0:T(8,128)} %query.1, f32[1,128,512]{2,1,0:T(8,128)} %keys.3, f32[1,128,512]{2,1,0:T(8,128)} %values.3, f32[3,128]{1,0:T(4,128)} %bitcast.7), custom_call_target="tpu_custom_call" | custom-call | flops 655360 | bytes 1590784 | tf_op jit(solution)/shard_map/pack/pallas_call | solution.py:361
  2.9 0.0 copy-start.4
  2.9 0.0 copy-start.6
  2.9 0.0 copy-start.7
  2.9 0.0 copy-start.8
  2.9 11.5 %all-to-all-start = ((f32[32,33,1,128]{3,2,1,0:T(1,128)}), f32[32,33,1,128]{3,2,1,0:T(1,128)S(1)}, u32[]{:S(2)}, u32[]{:S(2)}) async-start(f32[32,33,1,128]{3,2,1,0:T(1,128)} %bitcast.9), calls=%async_computation | async-start | bytes 1081344 | tf_op jit(solution)/shard_map/all_to_all | solution.py:379
  14.4 0.0 copy-done.4
  14.4 0.0 copy-done.6
  14.5 0.0 copy-done.7
  14.5 0.0 copy-done.8
  14.5 0.0 copy-start.5
  14.5 0.0 copy-start.9
  14.5 0.7 %filter_spectrum.1.filt = f32[512,256]{1,0:T(8,128)S(1)} custom-call(f32[4,16384]{1,0:T(4,128)S(1)} %copy-done.4, bf16[256,384]{1,0:T(8,128)(2,1)S(1)} %copy-done.7, bf16[512,256]{1,0:T(8,128)(2,1)S(1)} %copy-done.6, f32[128,256]{1,0:T(8,128)S(1)} %copy-done.8), custom_call_target="tpu_custom_call" | custom-call | flops 603979776 | bytes 1376256 | tf_op jit(solution)/shard_map/filter_spectrum/pallas_call | solution.py:361
  15.2 13.2 %all-to-all-done = f32[32,33,1,128]{3,2,1,0:T(1,128)S(1)} async-done(((f32[32,33,1,128]{3,2,1,0:T(1,128)}), f32[32,33,1,128]{3,2,1,0:T(1,128)S(1)}, u32[]{:S(2)}, u32[]{:S(2)}) %all-to-all-start) | async-done | bytes 540704 | tf_op jit(solution)/shard_map/all_to_all | solution.py:379
  28.5 0.0 copy-done.5
  28.5 0.0 copy-done.9
  28.5 2.7 %main.1 = (f32[1056,128]{1,0:T(8,128)}, f32[512,256]{1,0:T(8,128)S(1)}) custom-call(f32[1056,128]{1,0:T(8,128)S(1)} %bitcast.6, f32[512,256]{1,0:T(8,128)S(1)} %filter_spectrum.1.filt, bf16[256,384]{1,0:T(8,128)(2,1)S(1)} %copy-done.7, bf16[512,256]{1,0:T(8,128)(2,1)S(1)} %copy-done.6, bf16[512,256]{1,0:T(8,128)(2,1)S(1)} %copy-done.5, ...), custom_call_target="tpu_custom_call" | custom-call | flops 2415919104 | bytes 3112960 | tf_op jit(solution)/shard_map/main/pallas_call | solution.py:361
  31.2 7.9 %all-to-all-start.1 = ((f32[32,33,1,128]{3,2,1,0:T(1,128)}), f32[32,33,1,128]{3,2,1,0:T(1,128)S(1)}, u32[]{:S(2)}, u32[]{:S(2)}) async-start(f32[32,33,1,128]{3,2,1,0:T(1,128)} %bitcast.3), calls=%async_computation.1 | async-start | bytes 1081344 | tf_op jit(solution)/shard_map/all_to_all | solution.py:379
  39.1 0.0 copy-start
  39.1 0.0 copy-start.1
  39.1 0.0 copy-start.2
  39.1 0.0 copy-start.3
  39.1 0.7 %cross.1.part = f32[4,16384]{1,0:T(4,128)S(1)} custom-call(f32[512,256]{1,0:T(8,128)S(1)} %get-tuple-element.7.cross, bf16[512,256]{1,0:T(8,128)(2,1)S(1)} %copy-done.5, bf16[256,256]{1,0:T(8,128)(2,1)S(1)} %copy-done.9, f32[128,256]{1,0:T(8,128)S(1)} %copy-done.8), custom_call_target="tpu_custom_call" | custom-call | flops 603979776 | bytes 1310720 | tf_op jit(solution)/shard_map/cross/pallas_call | solution.py:361
  39.8 2.7 %collective-permute-start = (f32[4,16384]{1,0:T(4,128)S(1)}, f32[4,16384]{1,0:T(4,128)S(1)}, u32[]{:S(2)}, u32[]{:S(2)}) collective-permute-start(f32[4,16384]{1,0:T(4,128)S(1)} %cross.1.part), channel_id=1, source_target_pairs={{0,4},{4,0},{1,5},{5,1},{2,6},{6,2},{3,7},{7,3},{8,12},{12,8},{9,1... | collective-permute-start | bytes 786440 | tf_op jit(solution)/shard_map/ppermute | solution.py:444
  42.5 11.1 %collective-permute-done.other = f32[4,16384]{1,0:T(4,128)S(1)} collective-permute-done((f32[4,16384]{1,0:T(4,128)S(1)}, f32[4,16384]{1,0:T(4,128)S(1)}, u32[]{:S(2)}, u32[]{:S(2)}) %collective-permute-start) | collective-permute-done | bytes 262176 | tf_op jit(solution)/shard_map/ppermute | solution.py:444
  53.6 0.0 all-to-all-done.1
  53.6 0.0 copy-done
  53.6 0.0 copy-done.1
  53.6 0.0 copy-done.2
  53.7 0.0 copy-done.3
  53.7 1.3 %finish.1 = (f32[1,128,512]{2,1,0:T(8,128)}, f32[1,128,512]{2,1,0:T(8,128)}, f32[1,128,512]{2,1,0:T(8,128)}, f32[4,16384]{1,0:T(4,128)}) custom-call(f32[1056,128]{1,0:T(8,128)S(1)} %bitcast.5, f32[1,128,512]{2,1,0:T(8,128)S(1)} %copy-done, f32[1,128,512]{2,1,0:T(8,128)S(1)} %copy-done.1, f32[1,128,512]{2,1,0:T(8,128)S(1)} %copy-done.2, ...), custom_call_target="tpu_custom_call" | custom-call | flops 655360 | bytes 2901504 | tf_op jit(solution)/shard_map/finish/pallas_call | solution.py:361
Async XLA Ops:
  2.9 11.6 %copy-start.4 = (f32[4,16384]{1,0:T(4,128)S(1)}, f32[4,16384]{1,0:T(4,128)}, u32[]{:S(2)}) copy-start(f32[4,16384]{1,0:T(4,128)} %long_filter.1) | copy-start | bytes 786436
  2.9 11.6 %copy-start.6 = (bf16[512,256]{1,0:T(8,128)(2,1)S(1)}, bf16[512,256]{1,0:T(8,128)(2,1)}, u32[]{:S(2)}) copy-start(bf16[512,256]{1,0:T(8,128)(2,1)} %constant.11.clone.second) | copy-start | bytes 786436
  2.9 11.6 %copy-start.7 = (bf16[256,384]{1,0:T(8,128)(2,1)S(1)}, bf16[256,384]{1,0:T(8,128)(2,1)}, u32[]{:S(2)}) copy-start(bf16[256,384]{1,0:T(8,128)(2,1)} %constant.10.clone.first) | copy-start | bytes 589828
  2.9 11.6 %copy-start.8 = (f32[128,256]{1,0:T(8,128)S(1)}, f32[128,256]{1,0:T(8,128)}, u32[]{:S(2)}) copy-start(f32[128,256]{1,0:T(8,128)} %constant.14.clone.mid) | copy-start | bytes 393220
  2.9 25.6 %all-to-all-start = ((f32[32,33,1,128]{3,2,1,0:T(1,128)}), f32[32,33,1,128]{3,2,1,0:T(1,128)S(1)}, u32[]{:S(2)}, u32[]{:S(2)}) async-start(f32[32,33,1,128]{3,2,1,0:T(1,128)} %bitcast.9), calls=%async_computation | async-start | bytes 1081344 | tf_op jit(solution)/shard_map/all_to_all | solution.py:379
  14.5 14.0 %copy-start.5 = (bf16[512,256]{1,0:T(8,128)(2,1)S(1)}, bf16[512,256]{1,0:T(8,128)(2,1)}, u32[]{:S(2)}) copy-start(bf16[512,256]{1,0:T(8,128)(2,1)} %constant.12.clone.second_inv) | copy-start | bytes 786436
  14.5 14.0 %copy-start.9 = (bf16[256,256]{1,0:T(8,128)(2,1)S(1)}, bf16[256,256]{1,0:T(8,128)(2,1)}, u32[]{:S(2)}) copy-start(bf16[256,256]{1,0:T(8,128)(2,1)} %constant.13.clone.first_inv) | copy-start | bytes 393220
  31.2 22.4 %all-to-all-start.1 = ((f32[32,33,1,128]{3,2,1,0:T(1,128)}), f32[32,33,1,128]{3,2,1,0:T(1,128)S(1)}, u32[]{:S(2)}, u32[]{:S(2)}) async-start(f32[32,33,1,128]{3,2,1,0:T(1,128)} %bitcast.3), calls=%async_computation.1 | async-start | bytes 1081344 | tf_op jit(solution)/shard_map/all_to_all | solution.py:379
  39.1 14.6 %copy-start = (f32[1,128,512]{2,1,0:T(8,128)S(1)}, f32[1,128,512]{2,1,0:T(8,128)}, u32[]{:S(2)}) copy-start(f32[1,128,512]{2,1,0:T(8,128)} %grad_out.3) | copy-start | bytes 786436
  39.1 14.6 %copy-start.1 = (f32[1,128,512]{2,1,0:T(8,128)S(1)}, f32[1,128,512]{2,1,0:T(8,128)}, u32[]{:S(2)}) copy-start(f32[1,128,512]{2,1,0:T(8,128)} %keys.3) | copy-start | bytes 786436
  39.1 14.6 %copy-start.2 = (f32[1,128,512]{2,1,0:T(8,128)S(1)}, f32[1,128,512]{2,1,0:T(8,128)}, u32[]{:S(2)}) copy-start(f32[1,128,512]{2,1,0:T(8,128)} %values.3) | copy-start | bytes 786436
  39.1 14.6 %copy-start.3 = (f32[128,3]{0,1:T(4,128)S(1)}, f32[128,3]{0,1:T(4,128)}, u32[]{:S(2)}) copy-start(f32[128,3]{0,1:T(4,128)} %param.16) | copy-start | bytes 4612
  39.8 13.8 %collective-permute-start = (f32[4,16384]{1,0:T(4,128)S(1)}, f32[4,16384]{1,0:T(4,128)S(1)}, u32[]{:S(2)}, u32[]{:S(2)}) collective-permute-start(f32[4,16384]{1,0:T(4,128)S(1)} %cross.1.part), channel_id=1, source_target_pairs={{0,4},{4,0},{1,5},{5,1},{2,6},{6,2},{3,7},{7,3},{8,12},{12,8},{9,1... | collective-permute-start | bytes 786440 | tf_op jit(solution)/shard_map/ppermute | solution.py:444

commit v5 on v4

--- a/solution.py
+++ b/solution.py
@@ -25,7 +25,10 @@
 
 def peer_order(parts):
     planes = parts // CORES // 2
-    chips = [y * planes + z for z in reversed(range(planes)) for y in range(2)]
+    half = planes // 2
+    chips = [
+        y * planes + z + far for z in reversed(range(half)) for far in (half, 0) for y in range(2)
+    ]
     return [CORES * chip + core for chip in chips for core in range(CORES)]
 
 

time: 55.3 us -> 54.8 us (level)
  starting transfers between devices: 22.1 us -> 21 us
  waiting for transfers between devices: 24.3 us -> 25 us
    all_to_all x2, waiting for transfers between devices: 13.2 us -> 14.6 us  [exchange(): lax.all_to_all(moved, 'ctx', split_axis=0, concat_axis=0, axis_index_grou...]
    all_to_all x2, starting transfers between devices: 19.4 us -> 18.3 us  [exchange(): lax.all_to_all(moved, 'ctx', split_axis=0, concat_axis=0, axis_index_grou...]
    ppermute x1, waiting for transfers between devices: 11.1 us -> 10.4 us  [shards(): other = lax.ppermute(part, 'seq', [(0, 1), (1, 0)])]
  transfers between devices with their start and end apart: 3 -> 3, of which waited for: 2 -> 3; matrix products, arithmetic and copies ran while one was open for 0% -> 0% of each run, Pallas kernels for 3% -> 3%
where the time goes in v5:
time: 54.8 us; the launch traced here: 54.6 us
  waiting for transfers between devices  25 us (46%)
  starting transfers between devices  21 us (38%)
  Pallas kernels  7.72 us (14%)
  between operations  0.79 us (1%)
    all_to_all x2, starting transfers between devices, exchange(): lax.all_to_all(moved, 'ctx', split_axis=0, concat_axis=0, axis_index_grou...  18.3 us
    all_to_all x2, waiting for transfers between devices, exchange(): lax.all_to_all(moved, 'ctx', split_axis=0, concat_axis=0, axis_index_grou...  14.6 us
    ppermute x1, waiting for transfers between devices, shards(): other = lax.ppermute(part, 'seq', [(0, 1), (1, 0)])  10.4 us
    pallas_call x5, Pallas kernels, call(): pl.pallas_call(body, out_shape=outs, scratch_shapes=scratch, name=name, *...  7.72 us
    ppermute x1, starting transfers between devices, shards(): other = lax.ppermute(part, 'seq', [(0, 1), (1, 0)])  2.71 us
  transfers between devices with their start and end apart: 3, of which 3 were waited for; matrix products, arithmetic and copies ran while one was open for 0% of the time, Pallas kernels for 3%

profile of v5, /device:TPU:1, one launch (start us, length us, event | category | flops | bytes accessed | tf_op | source)
XLA Modules:
  0.0 54.6 jit_solution(1632951399381101772)
XLA Ops:
  0.6 2.2 %pack.1 = f32[1056,128]{1,0:T(8,128)} custom-call(f32[1,128,512]{2,1,0:T(8,128)} %grad_out.3, f32[1,128,512]{2,1,0:T(8,128)} %query.1, f32[1,128,512]{2,1,0:T(8,128)} %keys.3, f32[1,128,512]{2,1,0:T(8,128)} %values.3, f32[3,128]{1,0:T(4,128)} %bitcast.7), custom_call_target="tpu_custom_call" | custom-call | flops 655360 | bytes 1590784 | tf_op jit(solution)/shard_map/pack/pallas_call | solution.py:364
  2.9 0.0 copy-start.4
  2.9 0.0 copy-start.6
  2.9 0.0 copy-start.7
  2.9 0.0 copy-start.8
  2.9 11.5 %all-to-all-start = ((f32[32,33,1,128]{3,2,1,0:T(1,128)}), f32[32,33,1,128]{3,2,1,0:T(1,128)S(1)}, u32[]{:S(2)}, u32[]{:S(2)}) async-start(f32[32,33,1,128]{3,2,1,0:T(1,128)} %bitcast.9), calls=%async_computation | async-start | bytes 1081344 | tf_op jit(solution)/shard_map/all_to_all | solution.py:382
  14.4 0.0 copy-done.4
  14.4 0.0 copy-done.6
  14.5 0.0 copy-done.7
  14.5 0.0 copy-done.8
  14.5 0.0 copy-start.5
  14.5 0.0 copy-start.9
  14.5 0.7 %filter_spectrum.1.filt = f32[512,256]{1,0:T(8,128)S(1)} custom-call(f32[4,16384]{1,0:T(4,128)S(1)} %copy-done.4, bf16[256,384]{1,0:T(8,128)(2,1)S(1)} %copy-done.7, bf16[512,256]{1,0:T(8,128)(2,1)S(1)} %copy-done.6, f32[128,256]{1,0:T(8,128)S(1)} %copy-done.8), custom_call_target="tpu_custom_call" | custom-call | flops 603979776 | bytes 1376256 | tf_op jit(solution)/shard_map/filter_spectrum/pallas_call | solution.py:364
  15.2 13.9 %all-to-all-done = f32[32,33,1,128]{3,2,1,0:T(1,128)S(1)} async-done(((f32[32,33,1,128]{3,2,1,0:T(1,128)}), f32[32,33,1,128]{3,2,1,0:T(1,128)S(1)}, u32[]{:S(2)}, u32[]{:S(2)}) %all-to-all-start) | async-done | bytes 540704 | tf_op jit(solution)/shard_map/all_to_all | solution.py:382
  29.1 0.0 copy-done.5
  29.1 0.0 copy-done.9
  29.1 2.7 %main.1 = (f32[1056,128]{1,0:T(8,128)}, f32[512,256]{1,0:T(8,128)S(1)}) custom-call(f32[1056,128]{1,0:T(8,128)S(1)} %bitcast.6, f32[512,256]{1,0:T(8,128)S(1)} %filter_spectrum.1.filt, bf16[256,384]{1,0:T(8,128)(2,1)S(1)} %copy-done.7, bf16[512,256]{1,0:T(8,128)(2,1)S(1)} %copy-done.6, bf16[512,256]{1,0:T(8,128)(2,1)S(1)} %copy-done.5, ...), custom_call_target="tpu_custom_call" | custom-call | flops 2415919104 | bytes 3112960 | tf_op jit(solution)/shard_map/main/pallas_call | solution.py:364
  31.8 6.8 %all-to-all-start.1 = ((f32[32,33,1,128]{3,2,1,0:T(1,128)}), f32[32,33,1,128]{3,2,1,0:T(1,128)S(1)}, u32[]{:S(2)}, u32[]{:S(2)}) async-start(f32[32,33,1,128]{3,2,1,0:T(1,128)} %bitcast.3), calls=%async_computation.1 | async-start | bytes 1081344 | tf_op jit(solution)/shard_map/all_to_all | solution.py:382
  38.6 0.0 copy-start
  38.7 0.0 copy-start.1
  38.7 0.0 copy-start.2
  38.7 0.0 copy-start.3
  38.7 0.7 %cross.1.part = f32[4,16384]{1,0:T(4,128)S(1)} custom-call(f32[512,256]{1,0:T(8,128)S(1)} %get-tuple-element.7.cross, bf16[512,256]{1,0:T(8,128)(2,1)S(1)} %copy-done.5, bf16[256,256]{1,0:T(8,128)(2,1)S(1)} %copy-done.9, f32[128,256]{1,0:T(8,128)S(1)} %copy-done.8), custom_call_target="tpu_custom_call" | custom-call | flops 603979776 | bytes 1310720 | tf_op jit(solution)/shard_map/cross/pallas_call | solution.py:364
  39.4 2.7 %collective-permute-start = (f32[4,16384]{1,0:T(4,128)S(1)}, f32[4,16384]{1,0:T(4,128)S(1)}, u32[]{:S(2)}, u32[]{:S(2)}) collective-permute-start(f32[4,16384]{1,0:T(4,128)S(1)} %cross.1.part), channel_id=1, source_target_pairs={{0,4},{4,0},{1,5},{5,1},{2,6},{6,2},{3,7},{7,3},{8,12},{12,8},{9,1... | collective-permute-start | bytes 786440 | tf_op jit(solution)/shard_map/ppermute | solution.py:447
  42.1 10.4 %collective-permute-done.other = f32[4,16384]{1,0:T(4,128)S(1)} collective-permute-done((f32[4,16384]{1,0:T(4,128)S(1)}, f32[4,16384]{1,0:T(4,128)S(1)}, u32[]{:S(2)}, u32[]{:S(2)}) %collective-permute-start) | collective-permute-done | bytes 262176 | tf_op jit(solution)/shard_map/ppermute | solution.py:447
  52.5 0.7 %all-to-all-done.1 = f32[32,33,1,128]{3,2,1,0:T(1,128)S(1)} async-done(((f32[32,33,1,128]{3,2,1,0:T(1,128)}), f32[32,33,1,128]{3,2,1,0:T(1,128)S(1)}, u32[]{:S(2)}, u32[]{:S(2)}) %all-to-all-start.1) | async-done | bytes 540704 | tf_op jit(solution)/shard_map/all_to_all | solution.py:382
  53.2 0.0 copy-done
  53.2 0.0 copy-done.1
  53.2 0.0 copy-done.2
  53.2 0.0 copy-done.3
  53.2 1.3 %finish.1 = (f32[1,128,512]{2,1,0:T(8,128)}, f32[1,128,512]{2,1,0:T(8,128)}, f32[1,128,512]{2,1,0:T(8,128)}, f32[4,16384]{1,0:T(4,128)}) custom-call(f32[1056,128]{1,0:T(8,128)S(1)} %bitcast.5, f32[1,128,512]{2,1,0:T(8,128)S(1)} %copy-done, f32[1,128,512]{2,1,0:T(8,128)S(1)} %copy-done.1, f32[1,128,512]{2,1,0:T(8,128)S(1)} %copy-done.2, ...), custom_call_target="tpu_custom_call" | custom-call | flops 655360 | bytes 2901504 | tf_op jit(solution)/shard_map/finish/pallas_call | solution.py:364
Async XLA Ops:
  2.9 11.6 %copy-start.4 = (f32[4,16384]{1,0:T(4,128)S(1)}, f32[4,16384]{1,0:T(4,128)}, u32[]{:S(2)}) copy-start(f32[4,16384]{1,0:T(4,128)} %long_filter.1) | copy-start | bytes 786436
  2.9 11.6 %copy-start.6 = (bf16[512,256]{1,0:T(8,128)(2,1)S(1)}, bf16[512,256]{1,0:T(8,128)(2,1)}, u32[]{:S(2)}) copy-start(bf16[512,256]{1,0:T(8,128)(2,1)} %constant.11.clone.second) | copy-start | bytes 786436
  2.9 11.6 %copy-start.7 = (bf16[256,384]{1,0:T(8,128)(2,1)S(1)}, bf16[256,384]{1,0:T(8,128)(2,1)}, u32[]{:S(2)}) copy-start(bf16[256,384]{1,0:T(8,128)(2,1)} %constant.10.clone.first) | copy-start | bytes 589828
  2.9 11.6 %copy-start.8 = (f32[128,256]{1,0:T(8,128)S(1)}, f32[128,256]{1,0:T(8,128)}, u32[]{:S(2)}) copy-start(f32[128,256]{1,0:T(8,128)} %constant.14.clone.mid) | copy-start | bytes 393220
  2.9 26.2 %all-to-all-start = ((f32[32,33,1,128]{3,2,1,0:T(1,128)}), f32[32,33,1,128]{3,2,1,0:T(1,128)S(1)}, u32[]{:S(2)}, u32[]{:S(2)}) async-start(f32[32,33,1,128]{3,2,1,0:T(1,128)} %bitcast.9), calls=%async_computation | async-start | bytes 1081344 | tf_op jit(solution)/shard_map/all_to_all | solution.py:382
  14.5 14.6 %copy-start.5 = (bf16[512,256]{1,0:T(8,128)(2,1)S(1)}, bf16[512,256]{1,0:T(8,128)(2,1)}, u32[]{:S(2)}) copy-start(bf16[512,256]{1,0:T(8,128)(2,1)} %constant.12.clone.second_inv) | copy-start | bytes 786436
  14.5 14.6 %copy-start.9 = (bf16[256,256]{1,0:T(8,128)(2,1)S(1)}, bf16[256,256]{1,0:T(8,128)(2,1)}, u32[]{:S(2)}) copy-start(bf16[256,256]{1,0:T(8,128)(2,1)} %constant.13.clone.first_inv) | copy-start | bytes 393220
  31.8 21.4 %all-to-all-start.1 = ((f32[32,33,1,128]{3,2,1,0:T(1,128)}), f32[32,33,1,128]{3,2,1,0:T(1,128)S(1)}, u32[]{:S(2)}, u32[]{:S(2)}) async-start(f32[32,33,1,128]{3,2,1,0:T(1,128)} %bitcast.3), calls=%async_computation.1 | async-start | bytes 1081344 | tf_op jit(solution)/shard_map/all_to_all | solution.py:382
  38.6 14.6 %copy-start = (f32[1,128,512]{2,1,0:T(8,128)S(1)}, f32[1,128,512]{2,1,0:T(8,128)}, u32[]{:S(2)}) copy-start(f32[1,128,512]{2,1,0:T(8,128)} %grad_out.3) | copy-start | bytes 786436
  38.7 14.6 %copy-start.1 = (f32[1,128,512]{2,1,0:T(8,128)S(1)}, f32[1,128,512]{2,1,0:T(8,128)}, u32[]{:S(2)}) copy-start(f32[1,128,512]{2,1,0:T(8,128)} %keys.3) | copy-start | bytes 786436
  38.7 14.6 %copy-start.2 = (f32[1,128,512]{2,1,0:T(8,128)S(1)}, f32[1,128,512]{2,1,0:T(8,128)}, u32[]{:S(2)}) copy-start(f32[1,128,512]{2,1,0:T(8,128)} %values.3) | copy-start | bytes 786436
  38.7 14.5 %copy-start.3 = (f32[128,3]{0,1:T(4,128)S(1)}, f32[128,3]{0,1:T(4,128)}, u32[]{:S(2)}) copy-start(f32[128,3]{0,1:T(4,128)} %param.16) | copy-start | bytes 4612
  39.4 13.1 %collective-permute-start = (f32[4,16384]{1,0:T(4,128)S(1)}, f32[4,16384]{1,0:T(4,128)S(1)}, u32[]{:S(2)}, u32[]{:S(2)}) collective-permute-start(f32[4,16384]{1,0:T(4,128)S(1)} %cross.1.part), channel_id=1, source_target_pairs={{0,4},{4,0},{1,5},{5,1},{2,6},{6,2},{3,7},{7,3},{8,12},{12,8},{9,1... | collective-permute-start | bytes 786440 | tf_op jit(solution)/shard_map/ppermute | solution.py:447

commit v6 on v5

--- a/solution.py
+++ b/solution.py
@@ -36,10 +36,15 @@
     return [blocks * s + j for j in range(blocks) for s in order]
 
 
+def chip_order(order):
+    chips = [s // CORES for s in order[::CORES]]
+    assert [CORES * chip + core for chip in chips for core in range(CORES)] == list(order)
+    return chips
+
+
 def sorted_rows(x, order, own, back=False):
     size = CORES * own
-    chips = [s // CORES for s in order[::CORES]]
-    assert [CORES * chip + core for chip in chips for core in range(CORES)] == list(order)
+    chips = chip_order(order)
     if back:
         chips = [chips.index(k) for k in range(len(chips))]
     return jnp.concatenate([x[size * k : size * (k + 1)] for k in chips], 0)
@@ -166,51 +171,62 @@
 def pack_body(
     own, blocks, order, grad_out, query, keys, values, taps, out, held, few, scratch, edge, rows, sems
 ):
-    copies = [pltpu.make_async_copy(taps, few, sems.at[4])] + [
-        pltpu.make_async_copy(source.at[0], held.at[i], sems.at[i])
-        for i, source in enumerate((keys, values, grad_out, query))
-    ]
-    for copy in copies:
-        copy.start()
     chunk = 2 * own * blocks + 1
     chans, span = keys.shape[1:]
     peers = chans // own
-    copies[0].wait()
-    tap = tap_tiles(few)
-    copies[1].wait()
-    copies[2].wait()
-    key, value = held[0], held[1]
-    gated = short_taps(key, tap) * value
-    lane = lane_ids((chans, LANES))
-    tail = key[:, span - LANES :]
-    after = tap[2] * pltpu.roll(tail, 2, 1) + jnp.where(
-        lane < 1, tap[1] * pltpu.roll(tail, 1, 1), 0.0
-    )
-    head = jnp.where(lane < 4, pltpu.roll(value[:, :LANES], 2, 1), 0.0)
-    edge[...] = sorted_rows(jnp.where(lane < 2, after, head), order, own)
-    for j in range(blocks):
-        scratch[0, j] = sorted_rows(gated[:, j * LANES : (j + 1) * LANES], order, own)
-    copies[3].wait()
-    copies[4].wait()
-    for j in range(blocks):
-        here = slice(j * LANES, (j + 1) * LANES)
-        scratch[1, j] = sorted_rows(held[2, :, here] * held[3, :, here], order, own)
-    half = peers // 2
+    size, half = CORES * own, chans // 2
+    sources = (keys, values, grad_out, query)
+    chips = chip_order(order)
+    few_copy = pltpu.make_async_copy(taps, few, sems.at[8])
+    few_copy.start()
+    for h in range(2):
+        for i, source in enumerate(sources):
+            for k in range(h * half // size, (h + 1) * half // size):
+                pltpu.make_async_copy(
+                    source.at[0, pl.ds(size * chips[k], size)],
+                    held.at[i, pl.ds(size * k, size)],
+                    sems.at[2 * i + h],
+                ).start()
+    few_copy.wait()
+    tap = [sorted_rows(t, order, own) for t in tap_tiles(few)]
+    lane = lane_ids((half, LANES))
     writes = []
-    for part in range(2):
-        start = part * half * chunk
-        lines = lambda c: pl.ds(part * half * own + c, half, stride=own)
-        for t in range(2):
+    for h in range(2):
+        mine = pl.ds(h * half, half)
+        near = [t[h * half : (h + 1) * half] for t in tap]
+
+        def arrived(i):
+            pltpu.make_async_copy(
+                sources[i].at[0, pl.ds(0, half)], held.at[i, mine], sems.at[2 * i + h]
+            ).wait()
+
+        arrived(0)
+        arrived(1)
+        key, value = held[0, mine], held[1, mine]
+        gated = short_taps(key, near) * value
+        tail = key[:, span - LANES :]
+        after = near[2] * pltpu.roll(tail, 2, 1) + jnp.where(
+            lane < 1, near[1] * pltpu.roll(tail, 1, 1), 0.0
+        )
+        head = jnp.where(lane < 4, pltpu.roll(value[:, :LANES], 2, 1), 0.0)
+        edge[mine, :] = jnp.where(lane < 2, after, head)
+        arrived(2)
+        arrived(3)
+        grad = held[2, mine] * held[3, mine]
+        start = h * (peers // 2) * chunk
+        lines = lambda c: pl.ds(h * half + c, peers // 2, stride=own)
+        for t, whole in enumerate((gated, grad)):
             for j in range(blocks):
+                scratch[t, j, mine] = whole[:, j * LANES : (j + 1) * LANES]
                 for c in range(own):
                     place = start + 2 * own * j + own * t + c
-                    rows[pl.ds(place, half, stride=chunk), :] = scratch[t, j, lines(c), :]
+                    rows[pl.ds(place, peers // 2, stride=chunk), :] = scratch[t, j, lines(c), :]
         ends = edge[lines(0), :]
         for c in range(1, own):
             ends = ends + pltpu.roll(edge[lines(c), :], 4 * c, 1)
-        rows[pl.ds(start + chunk - 1, half, stride=chunk), :] = ends
-        piece = pl.ds(start, half * chunk)
-        writes.append(pltpu.make_async_copy(rows.at[piece], out.at[piece], sems.at[5 + part]))
+        rows[pl.ds(start + chunk - 1, peers // 2, stride=chunk), :] = ends
+        piece = pl.ds(start, peers // 2 * chunk)
+        writes.append(pltpu.make_async_copy(rows.at[piece], out.at[piece], sems.at[9 + h]))
         writes[-1].start()
     for write in writes:
         write.wait()
@@ -410,7 +426,7 @@
             tiles,
             pltpu.VMEM((chans, LANES), F32),
             pltpu.VMEM((packed_rows, LANES), F32),
-            pltpu.SemaphoreType.DMA((7,)),
+            pltpu.SemaphoreType.DMA((11,)),
         ],
         (grad_out, query, keys, values, taps),
         10 * chans * span,

time: 54.8 us -> 54.8 us (level)
  no operation moved by 1% of the time
where the time goes in v6:
time: 54.8 us; the launch traced here: 54.5 us
  waiting for transfers between devices  25 us (46%)
  starting transfers between devices  21 us (38%)
  Pallas kernels  7.65 us (14%)
  between operations  0.79 us (1%)
    all_to_all x2, starting transfers between devices, exchange(): lax.all_to_all(moved, 'ctx', split_axis=0, concat_axis=0, axis_index_grou...  18.3 us
    all_to_all x2, waiting for transfers between devices, exchange(): lax.all_to_all(moved, 'ctx', split_axis=0, concat_axis=0, axis_index_grou...  14.6 us
    ppermute x1, waiting for transfers between devices, shards(): other = lax.ppermute(part, 'seq', [(0, 1), (1, 0)])  10.4 us
    pallas_call x5, Pallas kernels, call(): pl.pallas_call(body, out_shape=outs, scratch_shapes=scratch, name=name, *...  7.65 us
    ppermute x1, starting transfers between devices, shards(): other = lax.ppermute(part, 'seq', [(0, 1), (1, 0)])  2.71 us
  transfers between devices with their start and end apart: 3, of which 3 were waited for; matrix products, arithmetic and copies ran while one was open for 0% of the time, Pallas kernels for 3%

profile of v6, /device:TPU:1, one launch (start us, length us, event | category | flops | bytes accessed | tf_op | source)
XLA Modules:
  0.0 54.5 jit_solution(18231877009268982026)
XLA Ops:
  0.6 2.1 %pack.1 = f32[1056,128]{1,0:T(8,128)} custom-call(f32[1,128,512]{2,1,0:T(8,128)} %grad_out.3, f32[1,128,512]{2,1,0:T(8,128)} %query.1, f32[1,128,512]{2,1,0:T(8,128)} %keys.3, f32[1,128,512]{2,1,0:T(8,128)} %values.3, f32[3,128]{1,0:T(4,128)} %bitcast.7), custom_call_target="tpu_custom_call" | custom-call | flops 655360 | bytes 1590784 | tf_op jit(solution)/shard_map/pack/pallas_call | solution.py:380
  2.8 0.0 copy-start.4
  2.8 0.0 copy-start.6
  2.8 0.0 copy-start.7
  2.8 0.0 copy-start.8
  2.8 11.5 %all-to-all-start = ((f32[32,33,1,128]{3,2,1,0:T(1,128)}), f32[32,33,1,128]{3,2,1,0:T(1,128)S(1)}, u32[]{:S(2)}, u32[]{:S(2)}) async-start(f32[32,33,1,128]{3,2,1,0:T(1,128)} %bitcast.9), calls=%async_computation | async-start | bytes 1081344 | tf_op jit(solution)/shard_map/all_to_all | solution.py:398
  14.4 0.0 copy-done.4
  14.4 0.0 copy-done.6
  14.4 0.0 copy-done.7
  14.4 0.0 copy-done.8
  14.4 0.0 copy-start.5
  14.4 0.0 copy-start.9
  14.4 0.7 %filter_spectrum.1.filt = f32[512,256]{1,0:T(8,128)S(1)} custom-call(f32[4,16384]{1,0:T(4,128)S(1)} %copy-done.4, bf16[256,384]{1,0:T(8,128)(2,1)S(1)} %copy-done.7, bf16[512,256]{1,0:T(8,128)(2,1)S(1)} %copy-done.6, f32[128,256]{1,0:T(8,128)S(1)} %copy-done.8), custom_call_target="tpu_custom_call" | custom-call | flops 603979776 | bytes 1376256 | tf_op jit(solution)/shard_map/filter_spectrum/pallas_call | solution.py:380
  15.2 13.9 %all-to-all-done = f32[32,33,1,128]{3,2,1,0:T(1,128)S(1)} async-done(((f32[32,33,1,128]{3,2,1,0:T(1,128)}), f32[32,33,1,128]{3,2,1,0:T(1,128)S(1)}, u32[]{:S(2)}, u32[]{:S(2)}) %all-to-all-start) | async-done | bytes 540704 | tf_op jit(solution)/shard_map/all_to_all | solution.py:398
  29.0 0.0 copy-done.5
  29.0 0.0 copy-done.9
  29.0 2.7 %main.1 = (f32[1056,128]{1,0:T(8,128)}, f32[512,256]{1,0:T(8,128)S(1)}) custom-call(f32[1056,128]{1,0:T(8,128)S(1)} %bitcast.6, f32[512,256]{1,0:T(8,128)S(1)} %filter_spectrum.1.filt, bf16[256,384]{1,0:T(8,128)(2,1)S(1)} %copy-done.7, bf16[512,256]{1,0:T(8,128)(2,1)S(1)} %copy-done.6, bf16[512,256]{1,0:T(8,128)(2,1)S(1)} %copy-done.5, ...), custom_call_target="tpu_custom_call" | custom-call | flops 2415919104 | bytes 3112960 | tf_op jit(solution)/shard_map/main/pallas_call | solution.py:380
  31.8 6.8 %all-to-all-start.1 = ((f32[32,33,1,128]{3,2,1,0:T(1,128)}), f32[32,33,1,128]{3,2,1,0:T(1,128)S(1)}, u32[]{:S(2)}, u32[]{:S(2)}) async-start(f32[32,33,1,128]{3,2,1,0:T(1,128)} %bitcast.3), calls=%async_computation.1 | async-start | bytes 1081344 | tf_op jit(solution)/shard_map/all_to_all | solution.py:398
  38.6 0.0 copy-start
  38.6 0.0 copy-start.1
  38.6 0.0 copy-start.2
  38.6 0.0 copy-start.3
  38.6 0.7 %cross.1.part = f32[4,16384]{1,0:T(4,128)S(1)} custom-call(f32[512,256]{1,0:T(8,128)S(1)} %get-tuple-element.7.cross, bf16[512,256]{1,0:T(8,128)(2,1)S(1)} %copy-done.5, bf16[256,256]{1,0:T(8,128)(2,1)S(1)} %copy-done.9, f32[128,256]{1,0:T(8,128)S(1)} %copy-done.8), custom_call_target="tpu_custom_call" | custom-call | flops 603979776 | bytes 1310720 | tf_op jit(solution)/shard_map/cross/pallas_call | solution.py:380
  39.3 2.7 %collective-permute-start = (f32[4,16384]{1,0:T(4,128)S(1)}, f32[4,16384]{1,0:T(4,128)S(1)}, u32[]{:S(2)}, u32[]{:S(2)}) collective-permute-start(f32[4,16384]{1,0:T(4,128)S(1)} %cross.1.part), channel_id=1, source_target_pairs={{0,4},{4,0},{1,5},{5,1},{2,6},{6,2},{3,7},{7,3},{8,12},{12,8},{9,1... | collective-permute-start | bytes 786440 | tf_op jit(solution)/shard_map/ppermute | solution.py:463
  42.0 10.4 %collective-permute-done.other = f32[4,16384]{1,0:T(4,128)S(1)} collective-permute-done((f32[4,16384]{1,0:T(4,128)S(1)}, f32[4,16384]{1,0:T(4,128)S(1)}, u32[]{:S(2)}, u32[]{:S(2)}) %collective-permute-start) | collective-permute-done | bytes 262176 | tf_op jit(solution)/shard_map/ppermute | solution.py:463
  52.4 0.7 %all-to-all-done.1 = f32[32,33,1,128]{3,2,1,0:T(1,128)S(1)} async-done(((f32[32,33,1,128]{3,2,1,0:T(1,128)}), f32[32,33,1,128]{3,2,1,0:T(1,128)S(1)}, u32[]{:S(2)}, u32[]{:S(2)}) %all-to-all-start.1) | async-done | bytes 540704 | tf_op jit(solution)/shard_map/all_to_all | solution.py:398
  53.1 0.0 copy-done
  53.1 0.0 copy-done.1
  53.1 0.0 copy-done.2
  53.2 0.0 copy-done.3
  53.2 1.3 %finish.1 = (f32[1,128,512]{2,1,0:T(8,128)}, f32[1,128,512]{2,1,0:T(8,128)}, f32[1,128,512]{2,1,0:T(8,128)}, f32[4,16384]{1,0:T(4,128)}) custom-call(f32[1056,128]{1,0:T(8,128)S(1)} %bitcast.5, f32[1,128,512]{2,1,0:T(8,128)S(1)} %copy-done, f32[1,128,512]{2,1,0:T(8,128)S(1)} %copy-done.1, f32[1,128,512]{2,1,0:T(8,128)S(1)} %copy-done.2, ...), custom_call_target="tpu_custom_call" | custom-call | flops 655360 | bytes 2901504 | tf_op jit(solution)/shard_map/finish/pallas_call | solution.py:380
Async XLA Ops:
  2.8 11.6 %copy-start.4 = (f32[4,16384]{1,0:T(4,128)S(1)}, f32[4,16384]{1,0:T(4,128)}, u32[]{:S(2)}) copy-start(f32[4,16384]{1,0:T(4,128)} %long_filter.1) | copy-start | bytes 786436
  2.8 11.6 %copy-start.6 = (bf16[512,256]{1,0:T(8,128)(2,1)S(1)}, bf16[512,256]{1,0:T(8,128)(2,1)}, u32[]{:S(2)}) copy-start(bf16[512,256]{1,0:T(8,128)(2,1)} %constant.11.clone.second) | copy-start | bytes 786436
  2.8 11.6 %copy-start.7 = (bf16[256,384]{1,0:T(8,128)(2,1)S(1)}, bf16[256,384]{1,0:T(8,128)(2,1)}, u32[]{:S(2)}) copy-start(bf16[256,384]{1,0:T(8,128)(2,1)} %constant.10.clone.first) | copy-start | bytes 589828
  2.8 11.6 %copy-start.8 = (f32[128,256]{1,0:T(8,128)S(1)}, f32[128,256]{1,0:T(8,128)}, u32[]{:S(2)}) copy-start(f32[128,256]{1,0:T(8,128)} %constant.14.clone.mid) | copy-start | bytes 393220
  2.8 26.2 %all-to-all-start = ((f32[32,33,1,128]{3,2,1,0:T(1,128)}), f32[32,33,1,128]{3,2,1,0:T(1,128)S(1)}, u32[]{:S(2)}, u32[]{:S(2)}) async-start(f32[32,33,1,128]{3,2,1,0:T(1,128)} %bitcast.9), calls=%async_computation | async-start | bytes 1081344 | tf_op jit(solution)/shard_map/all_to_all | solution.py:398
  14.4 14.6 %copy-start.5 = (bf16[512,256]{1,0:T(8,128)(2,1)S(1)}, bf16[512,256]{1,0:T(8,128)(2,1)}, u32[]{:S(2)}) copy-start(bf16[512,256]{1,0:T(8,128)(2,1)} %constant.12.clone.second_inv) | copy-start | bytes 786436
  14.4 14.6 %copy-start.9 = (bf16[256,256]{1,0:T(8,128)(2,1)S(1)}, bf16[256,256]{1,0:T(8,128)(2,1)}, u32[]{:S(2)}) copy-start(bf16[256,256]{1,0:T(8,128)(2,1)} %constant.13.clone.first_inv) | copy-start | bytes 393220
  31.8 21.4 %all-to-all-start.1 = ((f32[32,33,1,128]{3,2,1,0:T(1,128)}), f32[32,33,1,128]{3,2,1,0:T(1,128)S(1)}, u32[]{:S(2)}, u32[]{:S(2)}) async-start(f32[32,33,1,128]{3,2,1,0:T(1,128)} %bitcast.3), calls=%async_computation.1 | async-start | bytes 1081344 | tf_op jit(solution)/shard_map/all_to_all | solution.py:398
  38.6 14.6 %copy-start = (f32[1,128,512]{2,1,0:T(8,128)S(1)}, f32[1,128,512]{2,1,0:T(8,128)}, u32[]{:S(2)}) copy-start(f32[1,128,512]{2,1,0:T(8,128)} %grad_out.3) | copy-start | bytes 786436
  38.6 14.6 %copy-start.1 = (f32[1,128,512]{2,1,0:T(8,128)S(1)}, f32[1,128,512]{2,1,0:T(8,128)}, u32[]{:S(2)}) copy-start(f32[1,128,512]{2,1,0:T(8,128)} %keys.3) | copy-start | bytes 786436
  38.6 14.6 %copy-start.2 = (f32[1,128,512]{2,1,0:T(8,128)S(1)}, f32[1,128,512]{2,1,0:T(8,128)}, u32[]{:S(2)}) copy-start(f32[1,128,512]{2,1,0:T(8,128)} %values.3) | copy-start | bytes 786436
  38.6 14.6 %copy-start.3 = (f32[128,3]{0,1:T(4,128)S(1)}, f32[128,3]{0,1:T(4,128)}, u32[]{:S(2)}) copy-start(f32[128,3]{0,1:T(4,128)} %param.16) | copy-start | bytes 4612
  39.3 13.1 %collective-permute-start = (f32[4,16384]{1,0:T(4,128)S(1)}, f32[4,16384]{1,0:T(4,128)S(1)}, u32[]{:S(2)}, u32[]{:S(2)}) collective-permute-start(f32[4,16384]{1,0:T(4,128)S(1)} %cross.1.part), channel_id=1, source_target_pairs={{0,4},{4,0},{1,5},{5,1},{2,6},{6,2},{3,7},{7,3},{8,12},{12,8},{9,1... | collective-permute-start | bytes 786440 | tf_op jit(solution)/shard_map/ppermute | solution.py:463

commit v7 on v6

--- a/solution.py
+++ b/solution.py
@@ -210,12 +210,14 @@
         )
         head = jnp.where(lane < 4, pltpu.roll(value[:, :LANES], 2, 1), 0.0)
         edge[mine, :] = jnp.where(lane < 2, after, head)
-        arrived(2)
-        arrived(3)
-        grad = held[2, mine] * held[3, mine]
         start = h * (peers // 2) * chunk
         lines = lambda c: pl.ds(h * half + c, peers // 2, stride=own)
-        for t, whole in enumerate((gated, grad)):
+        for t in range(2):
+            whole = gated
+            if t:
+                arrived(2)
+                arrived(3)
+                whole = held[2, mine] * held[3, mine]
             for j in range(blocks):
                 scratch[t, j, mine] = whole[:, j * LANES : (j + 1) * LANES]
                 for c in range(own):

time: 54.8 us -> 54.8 us (level)
  no operation moved by 1% of the time
where the time goes in v7:
time: 54.8 us; the launch traced here: 54.5 us
  waiting for transfers between devices  24.9 us (45%)
  starting transfers between devices  21 us (38%)
  Pallas kernels  7.67 us (14%)
  between operations  0.79 us (1%)
    all_to_all x2, starting transfers between devices, exchange(): lax.all_to_all(moved, 'ctx', split_axis=0, concat_axis=0, axis_index_grou...  18.3 us
    all_to_all x2, waiting for transfers between devices, exchange(): lax.all_to_all(moved, 'ctx', split_axis=0, concat_axis=0, axis_index_grou...  14.6 us
    ppermute x1, waiting for transfers between devices, shards(): other = lax.ppermute(part, 'seq', [(0, 1), (1, 0)])  10.4 us
    pallas_call x5, Pallas kernels, call(): pl.pallas_call(body, out_shape=outs, scratch_shapes=scratch, name=name, *...  7.67 us
    ppermute x1, starting transfers between devices, shards(): other = lax.ppermute(part, 'seq', [(0, 1), (1, 0)])  2.71 us
  transfers between devices with their start and end apart: 3, of which 3 were waited for; matrix products, arithmetic and copies ran while one was open for 0% of the time, Pallas kernels for 3%

profile of v7, /device:TPU:1, one launch (start us, length us, event | category | flops | bytes accessed | tf_op | source)
XLA Modules:
  0.0 54.5 jit_solution(17106481428980529080)
XLA Ops:
  0.6 2.2 %pack.1 = f32[1056,128]{1,0:T(8,128)} custom-call(f32[1,128,512]{2,1,0:T(8,128)} %grad_out.3, f32[1,128,512]{2,1,0:T(8,128)} %query.1, f32[1,128,512]{2,1,0:T(8,128)} %keys.3, f32[1,128,512]{2,1,0:T(8,128)} %values.3, f32[3,128]{1,0:T(4,128)} %bitcast.7), custom_call_target="tpu_custom_call" | custom-call | flops 655360 | bytes 1590784 | tf_op jit(solution)/shard_map/pack/pallas_call | solution.py:382
  2.8 0.0 copy-start.4
  2.8 0.0 copy-start.6
  2.8 0.0 copy-start.7
  2.8 0.0 copy-start.8
  2.9 11.5 %all-to-all-start = ((f32[32,33,1,128]{3,2,1,0:T(1,128)}), f32[32,33,1,128]{3,2,1,0:T(1,128)S(1)}, u32[]{:S(2)}, u32[]{:S(2)}) async-start(f32[32,33,1,128]{3,2,1,0:T(1,128)} %bitcast.9), calls=%async_computation | async-start | bytes 1081344 | tf_op jit(solution)/shard_map/all_to_all | solution.py:400
  14.4 0.0 copy-done.4
  14.4 0.0 copy-done.6
  14.4 0.0 copy-done.7
  14.4 0.0 copy-done.8
  14.4 0.0 copy-start.5
  14.4 0.0 copy-start.9
  14.4 0.7 %filter_spectrum.1.filt = f32[512,256]{1,0:T(8,128)S(1)} custom-call(f32[4,16384]{1,0:T(4,128)S(1)} %copy-done.4, bf16[256,384]{1,0:T(8,128)(2,1)S(1)} %copy-done.7, bf16[512,256]{1,0:T(8,128)(2,1)S(1)} %copy-done.6, f32[128,256]{1,0:T(8,128)S(1)} %copy-done.8), custom_call_target="tpu_custom_call" | custom-call | flops 603979776 | bytes 1376256 | tf_op jit(solution)/shard_map/filter_spectrum/pallas_call | solution.py:382
  15.2 13.9 %all-to-all-done = f32[32,33,1,128]{3,2,1,0:T(1,128)S(1)} async-done(((f32[32,33,1,128]{3,2,1,0:T(1,128)}), f32[32,33,1,128]{3,2,1,0:T(1,128)S(1)}, u32[]{:S(2)}, u32[]{:S(2)}) %all-to-all-start) | async-done | bytes 540704 | tf_op jit(solution)/shard_map/all_to_all | solution.py:400
  29.1 0.0 copy-done.5
  29.1 0.0 copy-done.9
  29.1 2.7 %main.1 = (f32[1056,128]{1,0:T(8,128)}, f32[512,256]{1,0:T(8,128)S(1)}) custom-call(f32[1056,128]{1,0:T(8,128)S(1)} %bitcast.6, f32[512,256]{1,0:T(8,128)S(1)} %filter_spectrum.1.filt, bf16[256,384]{1,0:T(8,128)(2,1)S(1)} %copy-done.7, bf16[512,256]{1,0:T(8,128)(2,1)S(1)} %copy-done.6, bf16[512,256]{1,0:T(8,128)(2,1)S(1)} %copy-done.5, ...), custom_call_target="tpu_custom_call" | custom-call | flops 2415919104 | bytes 3112960 | tf_op jit(solution)/shard_map/main/pallas_call | solution.py:382
  31.8 6.8 %all-to-all-start.1 = ((f32[32,33,1,128]{3,2,1,0:T(1,128)}), f32[32,33,1,128]{3,2,1,0:T(1,128)S(1)}, u32[]{:S(2)}, u32[]{:S(2)}) async-start(f32[32,33,1,128]{3,2,1,0:T(1,128)} %bitcast.3), calls=%async_computation.1 | async-start | bytes 1081344 | tf_op jit(solution)/shard_map/all_to_all | solution.py:400
  38.6 0.0 copy-start
  38.6 0.0 copy-start.1
  38.6 0.0 copy-start.2
  38.6 0.0 copy-start.3
  38.6 0.7 %cross.1.part = f32[4,16384]{1,0:T(4,128)S(1)} custom-call(f32[512,256]{1,0:T(8,128)S(1)} %get-tuple-element.7.cross, bf16[512,256]{1,0:T(8,128)(2,1)S(1)} %copy-done.5, bf16[256,256]{1,0:T(8,128)(2,1)S(1)} %copy-done.9, f32[128,256]{1,0:T(8,128)S(1)} %copy-done.8), custom_call_target="tpu_custom_call" | custom-call | flops 603979776 | bytes 1310720 | tf_op jit(solution)/shard_map/cross/pallas_call | solution.py:382
  39.4 2.7 %collective-permute-start = (f32[4,16384]{1,0:T(4,128)S(1)}, f32[4,16384]{1,0:T(4,128)S(1)}, u32[]{:S(2)}, u32[]{:S(2)}) collective-permute-start(f32[4,16384]{1,0:T(4,128)S(1)} %cross.1.part), channel_id=1, source_target_pairs={{0,4},{4,0},{1,5},{5,1},{2,6},{6,2},{3,7},{7,3},{8,12},{12,8},{9,1... | collective-permute-start | bytes 786440 | tf_op jit(solution)/shard_map/ppermute | solution.py:465
  42.1 10.4 %collective-permute-done.other = f32[4,16384]{1,0:T(4,128)S(1)} collective-permute-done((f32[4,16384]{1,0:T(4,128)S(1)}, f32[4,16384]{1,0:T(4,128)S(1)}, u32[]{:S(2)}, u32[]{:S(2)}) %collective-permute-start) | collective-permute-done | bytes 262176 | tf_op jit(solution)/shard_map/ppermute | solution.py:465
  52.4 0.7 %all-to-all-done.1 = f32[32,33,1,128]{3,2,1,0:T(1,128)S(1)} async-done(((f32[32,33,1,128]{3,2,1,0:T(1,128)}), f32[32,33,1,128]{3,2,1,0:T(1,128)S(1)}, u32[]{:S(2)}, u32[]{:S(2)}) %all-to-all-start.1) | async-done | bytes 540704 | tf_op jit(solution)/shard_map/all_to_all | solution.py:400
  53.2 0.0 copy-done
  53.2 0.0 copy-done.1
  53.2 0.0 copy-done.2
  53.2 0.0 copy-done.3
  53.2 1.3 %finish.1 = (f32[1,128,512]{2,1,0:T(8,128)}, f32[1,128,512]{2,1,0:T(8,128)}, f32[1,128,512]{2,1,0:T(8,128)}, f32[4,16384]{1,0:T(4,128)}) custom-call(f32[1056,128]{1,0:T(8,128)S(1)} %bitcast.5, f32[1,128,512]{2,1,0:T(8,128)S(1)} %copy-done, f32[1,128,512]{2,1,0:T(8,128)S(1)} %copy-done.1, f32[1,128,512]{2,1,0:T(8,128)S(1)} %copy-done.2, ...), custom_call_target="tpu_custom_call" | custom-call | flops 655360 | bytes 2901504 | tf_op jit(solution)/shard_map/finish/pallas_call | solution.py:382
Async XLA Ops:
  2.8 11.6 %copy-start.4 = (f32[4,16384]{1,0:T(4,128)S(1)}, f32[4,16384]{1,0:T(4,128)}, u32[]{:S(2)}) copy-start(f32[4,16384]{1,0:T(4,128)} %long_filter.1) | copy-start | bytes 786436
  2.8 11.6 %copy-start.6 = (bf16[512,256]{1,0:T(8,128)(2,1)S(1)}, bf16[512,256]{1,0:T(8,128)(2,1)}, u32[]{:S(2)}) copy-start(bf16[512,256]{1,0:T(8,128)(2,1)} %constant.11.clone.second) | copy-start | bytes 786436
  2.8 11.6 %copy-start.7 = (bf16[256,384]{1,0:T(8,128)(2,1)S(1)}, bf16[256,384]{1,0:T(8,128)(2,1)}, u32[]{:S(2)}) copy-start(bf16[256,384]{1,0:T(8,128)(2,1)} %constant.10.clone.first) | copy-start | bytes 589828
  2.8 11.6 %copy-start.8 = (f32[128,256]{1,0:T(8,128)S(1)}, f32[128,256]{1,0:T(8,128)}, u32[]{:S(2)}) copy-start(f32[128,256]{1,0:T(8,128)} %constant.14.clone.mid) | copy-start | bytes 393220
  2.9 26.2 %all-to-all-start = ((f32[32,33,1,128]{3,2,1,0:T(1,128)}), f32[32,33,1,128]{3,2,1,0:T(1,128)S(1)}, u32[]{:S(2)}, u32[]{:S(2)}) async-start(f32[32,33,1,128]{3,2,1,0:T(1,128)} %bitcast.9), calls=%async_computation | async-start | bytes 1081344 | tf_op jit(solution)/shard_map/all_to_all | solution.py:400
  14.4 14.6 %copy-start.5 = (bf16[512,256]{1,0:T(8,128)(2,1)S(1)}, bf16[512,256]{1,0:T(8,128)(2,1)}, u32[]{:S(2)}) copy-start(bf16[512,256]{1,0:T(8,128)(2,1)} %constant.12.clone.second_inv) | copy-start | bytes 786436
  14.4 14.6 %copy-start.9 = (bf16[256,256]{1,0:T(8,128)(2,1)S(1)}, bf16[256,256]{1,0:T(8,128)(2,1)}, u32[]{:S(2)}) copy-start(bf16[256,256]{1,0:T(8,128)(2,1)} %constant.13.clone.first_inv) | copy-start | bytes 393220
  31.8 21.4 %all-to-all-start.1 = ((f32[32,33,1,128]{3,2,1,0:T(1,128)}), f32[32,33,1,128]{3,2,1,0:T(1,128)S(1)}, u32[]{:S(2)}, u32[]{:S(2)}) async-start(f32[32,33,1,128]{3,2,1,0:T(1,128)} %bitcast.3), calls=%async_computation.1 | async-start | bytes 1081344 | tf_op jit(solution)/shard_map/all_to_all | solution.py:400
  38.6 14.6 %copy-start = (f32[1,128,512]{2,1,0:T(8,128)S(1)}, f32[1,128,512]{2,1,0:T(8,128)}, u32[]{:S(2)}) copy-start(f32[1,128,512]{2,1,0:T(8,128)} %grad_out.3) | copy-start | bytes 786436
  38.6 14.6 %copy-start.1 = (f32[1,128,512]{2,1,0:T(8,128)S(1)}, f32[1,128,512]{2,1,0:T(8,128)}, u32[]{:S(2)}) copy-start(f32[1,128,512]{2,1,0:T(8,128)} %keys.3) | copy-start | bytes 786436
  38.6 14.6 %copy-start.2 = (f32[1,128,512]{2,1,0:T(8,128)S(1)}, f32[1,128,512]{2,1,0:T(8,128)}, u32[]{:S(2)}) copy-start(f32[1,128,512]{2,1,0:T(8,128)} %values.3) | copy-start | bytes 786436
  38.6 14.5 %copy-start.3 = (f32[128,3]{0,1:T(4,128)S(1)}, f32[128,3]{0,1:T(4,128)}, u32[]{:S(2)}) copy-start(f32[128,3]{0,1:T(4,128)} %param.16) | copy-start | bytes 4612
  39.4 13.1 %collective-permute-start = (f32[4,16384]{1,0:T(4,128)S(1)}, f32[4,16384]{1,0:T(4,128)S(1)}, u32[]{:S(2)}, u32[]{:S(2)}) collective-permute-start(f32[4,16384]{1,0:T(4,128)S(1)} %cross.1.part), channel_id=1, source_target_pairs={{0,4},{4,0},{1,5},{5,1},{2,6},{6,2},{3,7},{7,3},{8,12},{12,8},{9,1... | collective-permute-start | bytes 786440 | tf_op jit(solution)/shard_map/ppermute | solution.py:465
